TPU v7x, 256 devices: a whole 4x4x8 slice. The times are simulated.
256 devices in a mesh: dp: 4 (over y), mp: 16 (over x, z_lo), section: 4 (over z_hi, core).
Axes of the slice: x: 4, y: 4, z: 8 (z_hi: 2, z_lo: 4; z = z_hi * 4 + z_lo), core: 2. Of those that a mesh axis runs over, the one named last changes fastest.
Arguments:
- hidden_in: bfloat16 [64, 2560], P('dp', 'mp'), may hold values from -6 to 6
- lengths: int32 [64], P('dp'), may hold values from 0 to 7
- slots: int32 [64], P('dp'), may hold values from 0 to 71, as said below
- norm_gain: float32 [4, 2560], P('section'), may hold values from 0.5 to 1.5
- w_zxo: bfloat16 [4, 3, 5120, 2560], P('section', None, 'dp', 'mp'), may hold values from -0.125 to 0.125
- w_bcdt: bfloat16 [4, 336, 2560], P('section', 'dp', 'mp'), may hold values from -0.125 to 0.125
- conv_x_weight: float32 [4, 4, 5120], P('section', None, 'mp'), may hold values from -0.5 to 0.5
- conv_bc_weight: float32 [4, 4, 256], P('section'), may hold values from -0.5 to 0.5
- conv_x_pool: bfloat16 [4, 72, 3, 5120], P('section', 'dp', None, 'mp'), may hold values from -6 to 6
- conv_bc_pool: bfloat16 [4, 72, 3, 256], P('section', 'dp'), may hold values from -6 to 6
- state_pool: float32 [4, 72, 80, 64, 128], P('section', 'dp', 'mp'), may hold values from -1 to 1
- a_rate: float32 [4, 80], P('section', 'mp'), may hold values from 1 to 16
- dt_bias: float32 [4, 80], P('section', 'mp'), may hold values from -3 to 0
- skip_gain: float32 [4, 80], P('section', 'mp'), may hold values from 0.5 to 1.5
- gate_gain: float32 [4, 5120], P('section', 'mp'), may hold values from 0.5 to 1.5
Outputs:
- hidden_out: bfloat16 [4, 64, 2560], P('section', 'dp', 'mp')
- state_out: float32 [4, 64, 80, 64, 128], P('section', 'dp', 'mp')
Inputs may be any that keep to these rules, and one draw needn't show every extreme that they name: The sequences of the d-th block of 16 name distinct slots, all from d * 18 to (d + 1) * 18 - 1.
All inputs are finite; a program needn't handle non-finite values.
Results may differ from a plain program's by a relative error of at most 0.025.
Values may be sent and summed in bfloat16 or wider, within the bound.
A program may use at most 128 MiB of HBM per device.

v0:
```python
import jax
import jax.numpy as jnp
from jax import lax
from jax.sharding import PartitionSpec as P

MICRO = 4


epsilon = 1e-05


def copy_for_each(array, axis):
    devices = lax.axis_size(axis)
    return lax.all_to_all(
        jnp.broadcast_to(array[None], (devices, *array.shape)), axis, 0, 0, tiled=True
    )


def joined_along(tiles, dim):
    tiles = jnp.moveaxis(tiles, 0, dim)
    lengths = tiles.shape
    return tiles.reshape(*lengths[:dim], lengths[dim] * lengths[dim + 1], *lengths[dim + 2 :])


def gathered_copies(array, axis, dim):
    tiles = copy_for_each(array, axis)
    return joined_along(tiles, dim)


def over_copies(array, axis):
    return copy_for_each(array, axis).sum(axis=0)


def over_copies_2(array, axis):
    return copy_for_each(array, axis).astype(jnp.float32).sum(axis=0)


def passed_along(array, axis, by):
    devices = lax.axis_size(axis)
    pairs = [(i, i + by) for i in range(devices) if 0 <= i + by < devices]
    return lax.ppermute(array, axis, pairs)


def project(inputs, weights):
    return lax.dot_general(
        inputs, weights, (((1,), (1,)), ((), ())), preferred_element_type=jnp.float32
    )


def convolve(history, current, kernel, tap_mask):
    past_sum = jnp.sum(
        history.astype(jnp.float32) * tap_mask[:, :, None] * kernel[None, :3, :], axis=1
    )
    return jax.nn.silu(past_sum + current * kernel[3][None, :])


def local(
    hidden_in,
    lengths,
    slots,
    norm_gain,
    w_zxo,
    w_bcdt,
    conv_x_weight,
    conv_bc_weight,
    conv_x_pool,
    conv_bc_pool,
    state_pool,
    a_rate,
    dt_bias,
    skip_gain,
    gate_gain,
):
    section_index = lax.axis_index("section")
    section_count = lax.axis_size("section")
    mp_index = lax.axis_index("mp")
    mp_count = lax.axis_size("mp")
    dp_index = lax.axis_index("dp")
    seq_dev = hidden_in.shape[0]
    micro_rows = seq_dev // MICRO
    model_width = norm_gain.shape[1]
    model_share = hidden_in.shape[1]
    heads_dev = a_rate.shape[1]
    head_size = state_pool.shape[3]
    state_size = state_pool.shape[4]
    chan_dev = heads_dev * head_size
    slots_dev = state_pool.shape[1]
    bc_width = conv_bc_weight.shape[2]
    half_width = bc_width // 2
    zxo_rows, small_rows = (
        lax.all_gather(w_zxo, "dp", axis=2, tiled=True),
        lax.all_gather(w_bcdt[:, None], "dp", axis=2, tiled=True),
    )
    proj_weights = lax.all_to_all(zxo_rows, "mp", split_axis=2, concat_axis=3, tiled=True)[0]
    small_full = gathered_copies(small_rows, "mp", 3)[0, 0]
    entry_full = gathered_copies(hidden_in, "mp", 1)
    pre_gain = norm_gain[0]
    post_gain = gate_gain[0]
    kernel_x = conv_x_weight[0]
    kernel_bc = conv_bc_weight[0]
    rate_heads = a_rate[0]
    bias_heads = dt_bias[0]
    skip_heads = skip_gain[0]
    local_slots = slots - dp_index * slots_dev
    tick_count = MICRO + section_count - 1
    hidden_buffer = jnp.zeros((seq_dev, model_share), jnp.bfloat16)
    state_buffer = jnp.zeros((seq_dev, heads_dev, head_size, state_size), jnp.float32)
    received = None
    for tick_index in range(tick_count):
        if tick_index < MICRO:
            first_rows = entry_full[tick_index * micro_rows : (tick_index + 1) * micro_rows]
        else:
            first_rows = jnp.zeros((micro_rows, model_width), jnp.bfloat16)
        if tick_index == 0:
            layer_input = first_rows
        else:
            layer_input = jnp.where(section_index == 0, first_rows, received)
        micro_index = tick_index - section_index
        in_range = (micro_index >= 0) & (micro_index < MICRO)
        row_start = jnp.clip(micro_index, 0, MICRO - 1) * micro_rows
        rows_length = lax.dynamic_slice_in_dim(lengths, row_start, micro_rows)
        rows_slot = lax.dynamic_slice_in_dim(local_slots, row_start, micro_rows)
        tap_mask = (rows_length[:, None] >= (3 - jnp.arange(3, dtype=jnp.int32))[None, :]).astype(
            jnp.float32
        )
        alive = (rows_length > 0).astype(jnp.float32)
        residual = layer_input.astype(jnp.float32)
        normed_in = (
            residual
            * lax.rsqrt(jnp.mean(residual * residual, axis=1, keepdims=True) + epsilon)
            * pre_gain[None, :]
        ).astype(jnp.bfloat16)
        gate_proj = project(normed_in, proj_weights[0])
        inner_proj = project(normed_in, proj_weights[1])
        small_proj = project(normed_in, small_full)
        step_raw = lax.dynamic_slice_in_dim(
            small_proj, bc_width + mp_index * heads_dev, heads_dev, 1
        )
        conv_x = convolve(
            jnp.take(conv_x_pool[0], rows_slot, axis=0), inner_proj, kernel_x, tap_mask
        )
        conv_bc = convolve(
            jnp.take(conv_bc_pool[0], rows_slot, axis=0),
            small_proj[:, :bc_width],
            kernel_bc,
            tap_mask,
        )
        conv_b = conv_bc[:, :half_width]
        conv_c = conv_bc[:, half_width:]
        step_size = jax.nn.softplus(step_raw + bias_heads[None, :])
        decay_rate = jnp.exp(-step_size * rate_heads[None, :])
        old_state = jnp.take(state_pool[0], rows_slot, axis=0) * alive[:, None, None, None]
        inner_heads = conv_x.reshape(micro_rows, heads_dev, head_size)
        new_state = (
            decay_rate[:, :, None, None] * old_state
            + (step_size[:, :, None] * inner_heads)[:, :, :, None] * conv_b[:, None, None, :]
        )
        read_out = (
            jnp.einsum("bhpn,bn->bhp", new_state, conv_c, precision=lax.Precision.HIGHEST)
            + skip_heads[None, :, None] * inner_heads
        )
        gated = read_out.reshape(micro_rows, chan_dev) * jax.nn.silu(gate_proj)
        square_sum = over_copies(jnp.sum(gated * gated, axis=1), "mp")
        normed = (
            gated
            * lax.rsqrt(square_sum[:, None] / (chan_dev * mp_count) + epsilon)
            * post_gain[None, :]
        ).astype(jnp.bfloat16)
        partial_value = jnp.dot(normed, proj_weights[2], preferred_element_type=jnp.float32)
        summed = over_copies_2(partial_value.astype(jnp.bfloat16), "mp").astype(jnp.float32)
        new_full = (residual + summed).astype(jnp.bfloat16)
        new_share = lax.dynamic_slice_in_dim(new_full, mp_index * model_share, model_share, 1)
        current_hidden = lax.dynamic_slice_in_dim(hidden_buffer, row_start, micro_rows, 0)
        hidden_buffer = lax.dynamic_update_slice_in_dim(
            hidden_buffer, jnp.where(in_range, new_share, current_hidden), row_start, 0
        )
        current_state = lax.dynamic_slice_in_dim(state_buffer, row_start, micro_rows, 0)
        state_buffer = lax.dynamic_update_slice_in_dim(
            state_buffer, jnp.where(in_range, new_state, current_state), row_start, 0
        )
        if tick_index + 1 < tick_count:
            received = passed_along(new_full, "section", 1)
    return (hidden_buffer[None], state_buffer[None])


def solution(mesh):
    placed = (
        P("dp", "mp"),
        P("dp"),
        P("dp"),
        P("section", None),
        P("section", None, "dp", "mp"),
        P("section", "dp", "mp"),
        P("section", None, "mp"),
        P("section", None, None),
        P("section", "dp", None, "mp"),
        P("section", "dp", None, None),
        P("section", "dp", "mp", None, None),
        P("section", "mp"),
        P("section", "mp"),
        P("section", "mp"),
        P("section", "mp"),
    )
    return jax.shard_map(
        local,
        mesh=mesh,
        in_specs=placed,
        out_specs=(P("section", "dp", "mp"), P("section", "dp", "mp", None, None)),
        check_vma=False,
    )
```

profile of v0, /device:TPU:128, one launch (start us, length us, event | category | flops | bytes accessed | tf_op | source)
XLA Modules:
  0.0 585.2 jit_solution(429785838524593616)
XLA Ops:
  9.4 5.8 all-to-all-start
  16.1 13.6 %all-gather = bf16[1,336,160]{2,0,1:T(2,128)(2,1)S(1)} all-gather(bf16[1,84,160]{2,0,1:T(2,128)(2,1)S(1)} %copy.74), channel_id=2, replica_groups=mesh['dp'=4,'mp'=16,'section'=4] {'dp'}, dimensions={1}, use_global_device_ids=true | all-gather | bytes 134400 | tf_op jit(solution)/shard_map/all_gather | solution.py:92
  31.4 8.1 %all-to-all-start.1 = ((bf16[16,1,1,336,160]{3,4,2,1,0:T(8,128)(2,1)}), bf16[16,1,1,336,160]{3,4,2,1,0:T(8,128)(2,1)}, u32[]{:S(2)}, u32[]{:S(2)}) async-start(bf16[16,1,1,336,160]{3,4,2,1,0:T(8,128)(2,1)} %broadcast_in_dim.79), calls=%async_computation.1 | async-start | bytes 3932160 | tf_op jit(solution)/shard_map/all_to_all | solution.py:14
  39.5 29.2 %all-gather.3.cloned.1.call-done = bf16[1,3,5120,160]{2,3,1,0:T(8,128)(2,1)} async-done(((bf16[1,3,1280,160]{2,3,1,0:T(8,128)(2,1)}), bf16[1,3,5120,160]{2,3,1,0:T(8,128)(2,1)}) %all-gather.3.cloned.1.call-update) | async-done | bytes 4915216 | tf_op jit(solution)/shard_map/all_gather | solution.py:91
  68.6 15.5 %copy.76 = bf16[1,3,5120,160]{3,1,0,2:T(4,128)(2,1)} copy(bf16[1,3,5120,160]{2,3,1,0:T(8,128)(2,1)} %all-gather.3.cloned.1.call-done) | data formatting | bytes 9830400 | tf_op jit(solution)/shard_map/all_gather | solution.py:91
  84.1 17.6 %reshape.822 = bf16[16,2,76800]{2,1,0:T(2,128)(2,1)} reshape(bf16[5120,1,3,160]{3,2,1,0:T(4,128)(2,1)} %bitcast.134) | data formatting | bytes 9830400
  101.8 5.7 all-to-all-start.2
  117.6 101.7 %all-to-all-done.2 = bf16[16,2,76800]{2,1,0:T(2,128)(2,1)} async-done(((bf16[16,2,76800]{2,1,0:T(2,128)(2,1)}), bf16[16,2,76800]{2,1,0:T(2,128)(2,1)}, u32[]{:S(2)}, u32[]{:S(2)}) %all-to-all-start.2) | async-done | bytes 4915232 | tf_op jit(solution)/shard_map/all_to_all | solution.py:94
  219.2 17.3 %reshape.823 = bf16[5120,1,3,160]{3,2,1,0:T(4,128)(2,1)} reshape(bf16[16,2,76800]{2,1,0:T(2,128)(2,1)} %all-to-all-done.2) | data formatting | bytes 9830400
  236.5 17.8 %copy.77 = bf16[1,3,16,320,160]{3,4,2,1,0:T(8,128)(2,1)} copy(bf16[1,3,16,320,160]{4,1,3,2,0:T(4,128)(2,1)} %bitcast.135) | data formatting | bytes 9830400 | tf_op jit(solution)/shard_map/all_to_all | solution.py:94
  254.3 5.2 fusion.188
  261.4 2.7 fusion.21
  267.0 3.5 all-to-all-start.3
  271.1 7.1 %all-to-all-done.3 = f32[16,1,4]{2,1,0:T(1,128)S(1)} async-done(((f32[16,1,4]{2,1,0:T(1,128)}), f32[16,1,4]{2,1,0:T(1,128)S(1)}, u32[]{:S(2)}, u32[]{:S(2)}) %all-to-all-start.3) | async-done | bytes 288 | tf_op jit(solution)/shard_map/all_to_all | solution.py:14
  278.3 2.2 convolution_convert_fusion.6
  281.2 3.5 all-to-all-start.4
  309.9 3.8 collective-permute-done
  317.2 2.7 fusion.23
  320.1 2.1 multiply_reduce_fusion.21
  322.2 15.1 %all_to_all.102 = f32[16,1,4]{2,1,0:T(1,128)S(1)} all-to-all(f32[16,1,4]{2,1,0:T(1,128)S(1)} %broadcast_in_dim.82), channel_id=1, replica_groups=mesh['dp'=4,'mp'=16,'section'=4] {'mp'}, dimensions={0} | all-to-all | bytes 512 | tf_op jit(solution)/shard_map/all_to_all | solution.py:14
  337.3 2.2 convolution_convert_fusion.5
  339.6 12.8 %all_to_all.103 = bf16[16,4,2560]{2,1,0:T(4,128)(2,1)S(1)} all-to-all(bf16[16,4,2560]{2,1,0:T(4,128)(2,1)S(1)} %broadcast_in_dim.83), channel_id=1, replica_groups=mesh['dp'=4,'mp'=16,'section'=4] {'mp'}, dimensions={0} | all-to-all | bytes 655360 | tf_op jit(solution)/shard_map/all_to_all | solution.py:14
  356.2 5.4 collective-permute-done.1
  364.4 2.7 fusion.25
  367.3 2.1 multiply_reduce_fusion.20
  369.4 11.0 %all_to_all.104 = f32[16,1,4]{2,1,0:T(1,128)S(1)} all-to-all(f32[16,1,4]{2,1,0:T(1,128)S(1)} %broadcast_in_dim.84), channel_id=1, replica_groups=mesh['dp'=4,'mp'=16,'section'=4] {'mp'}, dimensions={0} | all-to-all | bytes 512 | tf_op jit(solution)/shard_map/all_to_all | solution.py:14
  380.5 2.2 convolution_convert_fusion.4
  382.7 12.6 %all_to_all.105 = bf16[16,4,2560]{2,1,0:T(4,128)(2,1)S(1)} all-to-all(bf16[16,4,2560]{2,1,0:T(4,128)(2,1)S(1)} %broadcast_in_dim.85), channel_id=1, replica_groups=mesh['dp'=4,'mp'=16,'section'=4] {'mp'}, dimensions={0} | all-to-all | bytes 655360 | tf_op jit(solution)/shard_map/all_to_all | solution.py:14
  399.1 5.4 collective-permute-done.2
  407.3 2.7 fusion.27
  410.2 2.1 multiply_reduce_fusion.19
  412.3 11.0 %all_to_all.106 = f32[16,1,4]{2,1,0:T(1,128)S(1)} all-to-all(f32[16,1,4]{2,1,0:T(1,128)S(1)} %broadcast_in_dim.86), channel_id=1, replica_groups=mesh['dp'=4,'mp'=16,'section'=4] {'mp'}, dimensions={0} | all-to-all | bytes 512 | tf_op jit(solution)/shard_map/all_to_all | solution.py:14
  423.4 2.2 convolution_convert_fusion.3
  426.4 3.5 all-to-all-start.10
  434.8 5.1 all-to-all-done.10
  440.1 2.1 collective-permute-start.3
  445.1 4.1 collective-permute-done.3
  454.0 2.1 multiply_reduce_fusion.18
  456.7 3.5 all-to-all-start.11
  460.9 7.0 %all-to-all-done.11 = f32[16,1,4]{2,1,0:T(1,128)S(1)} async-done(((f32[16,1,4]{2,1,0:T(1,128)}), f32[16,1,4]{2,1,0:T(1,128)S(1)}, u32[]{:S(2)}, u32[]{:S(2)}) %all-to-all-start.11) | async-done | bytes 288 | tf_op jit(solution)/shard_map/all_to_all | solution.py:14
  468.0 2.2 convolution_convert_fusion.2
  470.9 3.7 all-to-all-start.12
  474.7 2.5 select_dynamic-update-slice_fusion.4
  477.3 2.2 select_dynamic-update-slice_fusion.3
  479.6 5.0 all-to-all-done.12
  484.7 2.3 collective-permute-start.4
  487.0 2.4 select_dynamic-update-slice_fusion.2
  489.4 4.4 collective-permute-done.4
  498.6 2.1 multiply_reduce_fusion.17
  501.3 3.5 all-to-all-start.13
  504.9 7.6 %all-to-all-done.13 = f32[16,1,4]{2,1,0:T(1,128)S(1)} async-done(((f32[16,1,4]{2,1,0:T(1,128)}), f32[16,1,4]{2,1,0:T(1,128)S(1)}, u32[]{:S(2)}, u32[]{:S(2)}) %all-to-all-start.13) | async-done | bytes 288 | tf_op jit(solution)/shard_map/all_to_all | solution.py:14
  512.6 2.2 convolution_convert_fusion.1
  515.6 3.5 all-to-all-start.14
  519.2 2.5 select_dynamic-update-slice_fusion.1
  521.8 2.2 select_dynamic-update-slice_fusion
  524.0 3.6 copy.142
  531.3 7.0 %collective-permute-done.5 = bf16[4,2560]{1,0:T(4,128)(2,1)S(1)} collective-permute-done((bf16[4,2560]{1,0:T(4,128)(2,1)S(1)}, bf16[4,2560]{1,0:T(4,128)(2,1)S(1)}, u32[]{:S(2)}, u32[]{:S(2)}) %collective-permute-start.5) | collective-permute-done | bytes 20512 | tf_op jit(solution)/shard_map/ppermute | solution.py:41
  544.6 2.1 multiply_reduce_fusion.16
  547.3 5.9 %all-to-all-start.15 = ((f32[16,1,4]{2,1,0:T(1,128)}), f32[16,1,4]{2,1,0:T(1,128)S(1)}, u32[]{:S(2)}, u32[]{:S(2)}) async-start(f32[16,1,4]{2,1,0:T(1,128)} %broadcast_in_dim.93), calls=%async_computation.15 | async-start | bytes 16384 | tf_op jit(solution)/shard_map/all_to_all | solution.py:14
  553.2 2.4 bitcast_dynamic-update-slice_fusion
  555.6 5.4 all-to-all-done.15
  561.0 2.2 convolution_convert_fusion
  564.0 3.5 all-to-all-start.16
  567.6 9.9 %all-to-all-done.16 = bf16[16,4,2560]{2,1,0:T(4,128)(2,1)S(1)} async-done(((bf16[16,4,2560]{2,1,0:T(4,128)(2,1)}), bf16[16,4,2560]{2,1,0:T(4,128)(2,1)S(1)}, u32[]{:S(2)}, u32[]{:S(2)}) %all-to-all-start.16) | async-done | bytes 327712 | tf_op jit(solution)/shard_map/all_to_all | solution.py:14
  (351 shorter events, 97.9 us)
Async XLA Ops:
  7.2 104.1 %copy-start = (f32[1,18,5,64,128]{4,3,2,1,0:T(8,128)S(1)}, f32[1,18,5,64,128]{4,3,2,1,0:T(8,128)}, u32[]{:S(2)}) copy-start(f32[1,18,5,64,128]{4,3,2,1,0:T(8,128)} %param.31) | copy-start | bytes 8847364
  7.2 61.5 %all-gather.3.cloned.1.call-start = ((), (), s32[]{:S(2)}) async-start(), calls=%async_computation.17 | async-start | bytes 6144000 | tf_op jit(solution)/shard_map/all_gather | solution.py:91
  9.4 20.5 %all-to-all-start = ((bf16[16,16,160]{2,1,0:T(8,128)(2,1)}), bf16[16,16,160]{2,1,0:T(8,128)(2,1)S(1)}, u32[]{:S(2)}, u32[]{:S(2)}) async-start(bf16[16,16,160]{2,1,0:T(8,128)(2,1)} %broadcast_in_dim.76), calls=%async_computation | async-start | bytes 262144 | tf_op jit(solution)/shard_map/all_to_all | solution.py:14
  31.4 70.4 %all-to-all-start.1 = ((bf16[16,1,1,336,160]{3,4,2,1,0:T(8,128)(2,1)}), bf16[16,1,1,336,160]{3,4,2,1,0:T(8,128)(2,1)}, u32[]{:S(2)}, u32[]{:S(2)}) async-start(bf16[16,1,1,336,160]{3,4,2,1,0:T(8,128)(2,1)} %broadcast_in_dim.79), calls=%async_computation.1 | async-start | bytes 3932160 | tf_op jit(solution)/shard_map/all_to_all | solution.py:14
  101.7 5.7 copy-start.42
  101.8 5.9 %copy-start.75 = (s32[16]{0:T(128)S(1)}, s32[16]{0:T(128)}, u32[]{:S(2)}) copy-start(s32[16]{0:T(128)} %param.23) | copy-start | bytes 196
  101.8 5.9 %copy-start.27 = (s32[16]{0:T(128)S(1)}, s32[16]{0:T(128)}, u32[]{:S(2)}) copy-start(s32[16]{0:T(128)} %param.22) | copy-start | bytes 196
  101.8 9.4 %copy-start.62 = (f32[1,4,256]{2,1,0:T(4,128)S(1)}, f32[1,4,256]{2,1,0:T(4,128)}, u32[]{:S(2)}) copy-start(f32[1,4,256]{2,1,0:T(4,128)} %param.28) | copy-start | bytes 12292
  101.8 12.1 %copy-start.43 = (f32[1,4,320]{2,1,0:T(4,128)S(1)}, f32[1,4,320]{2,1,0:T(4,128)}, u32[]{:S(2)}) copy-start(f32[1,4,320]{2,1,0:T(4,128)} %param.27) | copy-start | bytes 15364
  101.8 117.4 %all-to-all-start.2 = ((bf16[16,2,76800]{2,1,0:T(2,128)(2,1)}), bf16[16,2,76800]{2,1,0:T(2,128)(2,1)}, u32[]{:S(2)}, u32[]{:S(2)}) async-start(bf16[16,2,76800]{2,1,0:T(2,128)(2,1)} %reshape.822), calls=%async_computation.2 | async-start | bytes 9830400 | tf_op jit(solution)/shard_map/all_to_all | solution.py:94
  108.4 153.0 %copy-start.59 = (pred[4]{0:T(512)(128)(4,1)}, pred[4]{0:T(512)(128)(4,1)S(1)}, u32[]{:S(2)}) copy-start(pred[4]{0:T(512)(128)(4,1)S(1)} %get-tuple-element.98) | copy-start | bytes 16
  108.4 153.0 %copy-start.71 = (f32[4]{0:T(128)}, f32[4]{0:T(128)S(1)}, u32[]{:S(2)}) copy-start(f32[4]{0:T(128)S(1)} %get-tuple-element.133) | copy-start | bytes 52
  108.4 9.0 %copy-start.28 = (f32[1,5]{1,0:T(1,128)S(1)}, f32[1,5]{1,0:T(1,128)}, u32[]{:S(2)}) copy-start(f32[1,5]{1,0:T(1,128)} %param.32) | copy-start | bytes 64
  108.4 9.0 %copy-start.30 = (f32[1,5]{1,0:T(1,128)S(1)}, f32[1,5]{1,0:T(1,128)}, u32[]{:S(2)}) copy-start(f32[1,5]{1,0:T(1,128)} %param.33) | copy-start | bytes 64
  111.2 125.2 %copy-start.18 = (f32[1,1,256]{2,1,0:T(1,128)}, f32[1,1,256]{2,1,0:T(1,128)S(1)}, u32[]{:S(2)}) copy-start(f32[1,1,256]{2,1,0:T(1,128)S(1)} %slice.161) | copy-start | bytes 3076
  113.9 145.7 %copy-start.15 = (f32[320]{0:T(512)}, f32[320]{0:T(512)S(1)}, u32[]{:S(2)}) copy-start(f32[320]{0:T(512)S(1)} %slice_reduce_fusion) | copy-start | bytes 3844
  114.6 187.6 %copy-start.39 = (f32[4,3]{1,0:T(4,128)}, f32[4,3]{1,0:T(4,128)S(1)}, u32[]{:S(2)}) copy-start(f32[4,3]{1,0:T(4,128)S(1)} %get-tuple-element.100) | copy-start | bytes 148
  117.5 143.9 %copy-start.51 = (f32[4,5]{1,0:T(4,128)}, f32[4,5]{1,0:T(4,128)S(1)}, u32[]{:S(2)}) copy-start(f32[4,5]{1,0:T(4,128)S(1)} %get-tuple-element.61) | copy-start | bytes 244
  117.5 143.8 %copy-start.53 = (f32[4,128]{1,0:T(4,128)}, f32[4,128]{1,0:T(4,128)S(1)}, u32[]{:S(2)}) copy-start(f32[4,128]{1,0:T(4,128)S(1)} %get-tuple-element.86) | copy-start | bytes 6148
  259.5 4.6 copy-start.25
  261.2 9.9 %copy-start.74 = (f32[1,320]{1,0:T(1,128)S(1)}, f32[1,320]{1,0:T(1,128)}, u32[]{:S(2)}) copy-start(f32[1,320]{1,0:T(1,128)} %param.35) | copy-start | bytes 3844
  266.4 18.4 %copy-start.73 = (s32[4]{0:T(128)S(1)}, s32[4]{0:T(128)}, u32[]{:S(2)}) copy-start(s32[4]{0:T(128)} %get-tuple-element.91) | copy-start | bytes 52
  266.4 19.0 %copy-start.13 = (bf16[1,18,3,320]{3,2,1,0:T(4,128)(2,1)S(1)}, bf16[1,18,3,320]{3,2,1,0:T(4,128)(2,1)}, u32[]{:S(2)}) copy-start(bf16[1,18,3,320]{3,2,1,0:T(4,128)(2,1)} %param.29) | copy-start | bytes 103684
  266.4 19.7 %copy-start.17 = (bf16[1,18,3,256]{3,2,1,0:T(4,128)(2,1)S(1)}, bf16[1,18,3,256]{3,2,1,0:T(4,128)(2,1)}, u32[]{:S(2)}) copy-start(bf16[1,18,3,256]{3,2,1,0:T(4,128)(2,1)} %param.30) | copy-start | bytes 82948
  266.4 35.8 %copy-start.23 = (f32[3,320]{1,0:T(4,128)S(1)}, f32[3,320]{1,0:T(4,128)}, u32[]{:S(2)}) copy-start(f32[3,320]{1,0:T(4,128)} %copy-done.22) | copy-start | bytes 11524
  267.0 11.2 %all-to-all-start.3 = ((f32[16,1,4]{2,1,0:T(1,128)}), f32[16,1,4]{2,1,0:T(1,128)S(1)}, u32[]{:S(2)}, u32[]{:S(2)}) async-start(f32[16,1,4]{2,1,0:T(1,128)} %broadcast_in_dim.80), calls=%async_computation.3 | async-start | bytes 16384 | tf_op jit(solution)/shard_map/all_to_all | solution.py:14
  281.2 23.3 %all-to-all-start.4 = ((bf16[16,4,2560]{2,1,0:T(4,128)(2,1)}), bf16[16,4,2560]{2,1,0:T(4,128)(2,1)S(1)}, u32[]{:S(2)}, u32[]{:S(2)}) async-start(bf16[16,4,2560]{2,1,0:T(4,128)(2,1)} %broadcast_in_dim.81), calls=%async_computation.4 | async-start | bytes 655360 | tf_op jit(solution)/shard_map/all_to_all | solution.py:14
  304.4 5.4 copy-start.14
  304.5 11.4 %copy-start.16 = (f32[320]{0:T(512)S(1)}, f32[320]{0:T(512)}, u32[]{:S(2)}) copy-start(f32[320]{0:T(512)} %copy-done.15) | copy-start | bytes 3844
  304.5 11.4 %copy-start.38 = (f32[4,320]{1,0:T(4,128)S(1)}, f32[4,320]{1,0:T(4,128)}, u32[]{:S(2)}) copy-start(f32[4,320]{1,0:T(4,128)} %get-tuple-element.6) | copy-start | bytes 15364
  304.7 11.6 %copy-start.32 = (bf16[4,2560]{1,0:T(4,128)(2,1)}, bf16[4,2560]{1,0:T(4,128)(2,1)S(1)}, u32[]{:S(2)}) copy-start(bf16[4,2560]{1,0:T(4,128)(2,1)S(1)} %add_convert_fusion) | copy-start | bytes 61444
  304.7 9.0 %collective-permute-start = (bf16[4,2560]{1,0:T(4,128)(2,1)S(1)}, bf16[4,2560]{1,0:T(4,128)(2,1)S(1)}, u32[]{:S(2)}, u32[]{:S(2)}) collective-permute-start(bf16[4,2560]{1,0:T(4,128)(2,1)S(1)} %add_convert_fusion), channel_id=1, source_target_pairs={{0,1},{1,2},{2,3},{4,5},{5,6},{6,7},{8,9},{9,10},{10,11},{12,13},{... | collective-permute-start | bytes 61448 | tf_op jit(solution)/shard_map/ppermute | solution.py:41
  309.9 6.0 %copy-start.2 = (bf16[1,1,320,16,160]{2,4,3,1,0:T(8,128)(2,1)S(1)}, bf16[1,1,320,16,160]{2,4,3,1,0:T(8,128)(2,1)}, u32[]{:S(2)}) copy-start(bf16[1,1,320,16,160]{2,4,3,1,0:T(8,128)(2,1)} %copy-done.1) | copy-start | bytes 4915204
  352.4 11.3 %copy-start.37 = (f32[4,320]{1,0:T(4,128)S(1)}, f32[4,320]{1,0:T(4,128)}, u32[]{:S(2)}) copy-start(f32[4,320]{1,0:T(4,128)} %get-tuple-element.7) | copy-start | bytes 15364
  352.5 9.0 %collective-permute-start.1 = (bf16[4,2560]{1,0:T(4,128)(2,1)S(1)}, bf16[4,2560]{1,0:T(4,128)(2,1)S(1)}, u32[]{:S(2)}, u32[]{:S(2)}) collective-permute-start(bf16[4,2560]{1,0:T(4,128)(2,1)S(1)} %fusion.80), channel_id=1, source_target_pairs={{0,1},{1,2},{2,3},{4,5},{5,6},{6,7},{8,9},{9,10},{10,11},{12,13},{... | collective-permute-start | bytes 61448 | tf_op jit(solution)/shard_map/ppermute | solution.py:41
  356.2 7.5 %copy-start.3 = (bf16[1,1,320,16,160]{2,4,3,1,0:T(8,128)(2,1)S(1)}, bf16[1,1,320,16,160]{2,4,3,1,0:T(8,128)(2,1)}, u32[]{:S(2)}) copy-start(bf16[1,1,320,16,160]{2,4,3,1,0:T(8,128)(2,1)} %copy-done.1) | copy-start | bytes 4915204
  395.3 11.3 %copy-start.36 = (f32[4,320]{1,0:T(4,128)S(1)}, f32[4,320]{1,0:T(4,128)}, u32[]{:S(2)}) copy-start(f32[4,320]{1,0:T(4,128)} %get-tuple-element.8) | copy-start | bytes 15364
  395.5 9.0 %collective-permute-start.2 = (bf16[4,2560]{1,0:T(4,128)(2,1)S(1)}, bf16[4,2560]{1,0:T(4,128)(2,1)S(1)}, u32[]{:S(2)}, u32[]{:S(2)}) collective-permute-start(bf16[4,2560]{1,0:T(4,128)(2,1)S(1)} %fusion.84), channel_id=1, source_target_pairs={{0,1},{1,2},{2,3},{4,5},{5,6},{6,7},{8,9},{9,10},{10,11},{12,13},{... | collective-permute-start | bytes 61448 | tf_op jit(solution)/shard_map/ppermute | solution.py:41
  399.0 7.6 %copy-start.4 = (bf16[1,1,320,16,160]{2,4,3,1,0:T(8,128)(2,1)S(1)}, bf16[1,1,320,16,160]{2,4,3,1,0:T(8,128)(2,1)}, u32[]{:S(2)}) copy-start(bf16[1,1,320,16,160]{2,4,3,1,0:T(8,128)(2,1)} %copy-done.1) | copy-start | bytes 4915204
  426.4 13.5 %all-to-all-start.10 = ((bf16[16,4,2560]{2,1,0:T(4,128)(2,1)}), bf16[16,4,2560]{2,1,0:T(4,128)(2,1)S(1)}, u32[]{:S(2)}, u32[]{:S(2)}) async-start(bf16[16,4,2560]{2,1,0:T(4,128)(2,1)} %broadcast_in_dim.87), calls=%async_computation.10 | async-start | bytes 655360 | tf_op jit(solution)/shard_map/all_to_all | solution.py:14
  433.1 10.9 %copy-start.21 = (f32[4,5,64]{2,1,0:T(8,128)S(1)}, f32[4,5,64]{2,1,0:T(8,128)}, u32[]{:S(2)}) copy-start(f32[4,5,64]{2,1,0:T(8,128)} %copy-done.20) | copy-start | bytes 15364
  433.1 10.9 %copy-start.52 = (f32[4,5]{1,0:T(4,128)S(1)}, f32[4,5]{1,0:T(4,128)}, u32[]{:S(2)}) copy-start(f32[4,5]{1,0:T(4,128)} %copy-done.51) | copy-start | bytes 244
  433.1 10.9 %copy-start.54 = (f32[4,128]{1,0:T(4,128)S(1)}, f32[4,128]{1,0:T(4,128)}, u32[]{:S(2)}) copy-start(f32[4,128]{1,0:T(4,128)} %copy-done.53) | copy-start | bytes 6148
  433.1 10.9 %copy-start.60 = (pred[4]{0:T(512)(128)(4,1)S(1)}, pred[4]{0:T(512)(128)(4,1)}, u32[]{:S(2)}) copy-start(pred[4]{0:T(512)(128)(4,1)} %copy-done.59) | copy-start | bytes 16
  433.1 10.9 %copy-start.72 = (f32[4]{0:T(128)S(1)}, f32[4]{0:T(128)}, u32[]{:S(2)}) copy-start(f32[4]{0:T(128)} %copy-done.71) | copy-start | bytes 52
  440.0 9.3 %copy-start.5 = (bf16[1,1,320,16,160]{2,4,3,1,0:T(8,128)(2,1)S(1)}, bf16[1,1,320,16,160]{2,4,3,1,0:T(8,128)(2,1)}, u32[]{:S(2)}) copy-start(bf16[1,1,320,16,160]{2,4,3,1,0:T(8,128)(2,1)} %copy-done.1) | copy-start | bytes 4915204
  440.1 9.3 %copy-start.35 = (f32[4,320]{1,0:T(4,128)S(1)}, f32[4,320]{1,0:T(4,128)}, u32[]{:S(2)}) copy-start(f32[4,320]{1,0:T(4,128)} %get-tuple-element.9) | copy-start | bytes 15364
  440.1 9.1 %collective-permute-start.3 = (bf16[4,2560]{1,0:T(4,128)(2,1)S(1)}, bf16[4,2560]{1,0:T(4,128)(2,1)S(1)}, u32[]{:S(2)}, u32[]{:S(2)}) collective-permute-start(bf16[4,2560]{1,0:T(4,128)(2,1)S(1)} %fusion.88), channel_id=1, source_target_pairs={{0,1},{1,2},{2,3},{4,5},{5,6},{6,7},{8,9},{9,10},{10,11},{12,13},{... | collective-permute-start | bytes 61448 | tf_op jit(solution)/shard_map/ppermute | solution.py:41
  456.1 18.6 %copy-start.50 = (pred[4]{0:T(512)(128)(4,1)S(1)}, pred[4]{0:T(512)(128)(4,1)}, u32[]{:S(2)}) copy-start(pred[4]{0:T(512)(128)(4,1)} %get-tuple-element.96) | copy-start | bytes 16
  456.1 18.6 %copy-start.56 = (f32[4,5]{1,0:T(4,128)S(1)}, f32[4,5]{1,0:T(4,128)}, u32[]{:S(2)}) copy-start(f32[4,5]{1,0:T(4,128)} %copy-done.55) | copy-start | bytes 244
  456.1 18.6 %copy-start.58 = (f32[4,128]{1,0:T(4,128)S(1)}, f32[4,128]{1,0:T(4,128)}, u32[]{:S(2)}) copy-start(f32[4,128]{1,0:T(4,128)} %copy-done.57) | copy-start | bytes 6148
  456.7 11.2 %all-to-all-start.11 = ((f32[16,1,4]{2,1,0:T(1,128)}), f32[16,1,4]{2,1,0:T(1,128)S(1)}, u32[]{:S(2)}, u32[]{:S(2)}) async-start(f32[16,1,4]{2,1,0:T(1,128)} %broadcast_in_dim.88), calls=%async_computation.11 | async-start | bytes 16384 | tf_op jit(solution)/shard_map/all_to_all | solution.py:14
  470.9 6.3 %copy-start.69 = (f32[4]{0:T(128)S(1)}, f32[4]{0:T(128)}, u32[]{:S(2)}) copy-start(f32[4]{0:T(128)} %get-tuple-element.137) | copy-start | bytes 52
  470.9 13.6 %all-to-all-start.12 = ((bf16[16,4,2560]{2,1,0:T(4,128)(2,1)}), bf16[16,4,2560]{2,1,0:T(4,128)(2,1)S(1)}, u32[]{:S(2)}, u32[]{:S(2)}) async-start(bf16[16,4,2560]{2,1,0:T(4,128)(2,1)} %broadcast_in_dim.89), calls=%async_computation.12 | async-start | bytes 655360 | tf_op jit(solution)/shard_map/all_to_all | solution.py:14
  474.7 12.3 %copy-start.67 = (f32[4]{0:T(128)S(1)}, f32[4]{0:T(128)}, u32[]{:S(2)}) copy-start(f32[4]{0:T(128)} %get-tuple-element.139) | copy-start | bytes 52
  477.3 16.8 %copy-start.34 = (f32[4,320]{1,0:T(4,128)S(1)}, f32[4,320]{1,0:T(4,128)}, u32[]{:S(2)}) copy-start(f32[4,320]{1,0:T(4,128)} %get-tuple-element.10) | copy-start | bytes 15364
  484.6 9.5 %copy-start.6 = (bf16[1,1,320,16,160]{2,4,3,1,0:T(8,128)(2,1)S(1)}, bf16[1,1,320,16,160]{2,4,3,1,0:T(8,128)(2,1)}, u32[]{:S(2)}) copy-start(bf16[1,1,320,16,160]{2,4,3,1,0:T(8,128)(2,1)} %copy-done.1) | copy-start | bytes 4915204
  484.7 9.1 %collective-permute-start.4 = (bf16[4,2560]{1,0:T(4,128)(2,1)S(1)}, bf16[4,2560]{1,0:T(4,128)(2,1)S(1)}, u32[]{:S(2)}, u32[]{:S(2)}) collective-permute-start(bf16[4,2560]{1,0:T(4,128)(2,1)S(1)} %fusion.92), channel_id=1, source_target_pairs={{0,1},{1,2},{2,3},{4,5},{5,6},{6,7},{8,9},{9,10},{10,11},{12,13},{... | collective-permute-start | bytes 61448 | tf_op jit(solution)/shard_map/ppermute | solution.py:41
  501.3 11.2 %all-to-all-start.13 = ((f32[16,1,4]{2,1,0:T(1,128)}), f32[16,1,4]{2,1,0:T(1,128)S(1)}, u32[]{:S(2)}, u32[]{:S(2)}) async-start(f32[16,1,4]{2,1,0:T(1,128)} %broadcast_in_dim.90), calls=%async_computation.13 | async-start | bytes 16384 | tf_op jit(solution)/shard_map/all_to_all | solution.py:14
  515.6 13.5 %all-to-all-start.14 = ((bf16[16,4,2560]{2,1,0:T(4,128)(2,1)}), bf16[16,4,2560]{2,1,0:T(4,128)(2,1)S(1)}, u32[]{:S(2)}, u32[]{:S(2)}) async-start(bf16[16,4,2560]{2,1,0:T(4,128)(2,1)} %broadcast_in_dim.91), calls=%async_computation.14 | async-start | bytes 655360 | tf_op jit(solution)/shard_map/all_to_all | solution.py:14
  524.0 14.5 %copy-start.33 = (f32[4,320]{1,0:T(4,128)S(1)}, f32[4,320]{1,0:T(4,128)}, u32[]{:S(2)}) copy-start(f32[4,320]{1,0:T(4,128)} %get-tuple-element.4) | copy-start | bytes 15364
  529.3 9.0 %collective-permute-start.5 = (bf16[4,2560]{1,0:T(4,128)(2,1)S(1)}, bf16[4,2560]{1,0:T(4,128)(2,1)S(1)}, u32[]{:S(2)}, u32[]{:S(2)}) collective-permute-start(bf16[4,2560]{1,0:T(4,128)(2,1)S(1)} %fusion.96), channel_id=1, source_target_pairs={{0,1},{1,2},{2,3},{4,5},{5,6},{6,7},{8,9},{9,10},{10,11},{12,13},{... | collective-permute-start | bytes 61448 | tf_op jit(solution)/shard_map/ppermute | solution.py:41
  547.3 13.7 %all-to-all-start.15 = ((f32[16,1,4]{2,1,0:T(1,128)}), f32[16,1,4]{2,1,0:T(1,128)S(1)}, u32[]{:S(2)}, u32[]{:S(2)}) async-start(f32[16,1,4]{2,1,0:T(1,128)} %broadcast_in_dim.93), calls=%async_computation.15 | async-start | bytes 16384 | tf_op jit(solution)/shard_map/all_to_all | solution.py:14
  564.0 13.5 %all-to-all-start.16 = ((bf16[16,4,2560]{2,1,0:T(4,128)(2,1)}), bf16[16,4,2560]{2,1,0:T(4,128)(2,1)S(1)}, u32[]{:S(2)}, u32[]{:S(2)}) async-start(bf16[16,4,2560]{2,1,0:T(4,128)(2,1)} %broadcast_in_dim.94), calls=%async_computation.16 | async-start | bytes 655360 | tf_op jit(solution)/shard_map/all_to_all | solution.py:14
  (31 other events, 79.0 us)
Sparse Core Ops, SparseCore 0:
  9.8 58.7 all-gather.2
where the time goes:
time: 590 us; the launch traced here: 585 us
  waiting for transfers between devices  210 us (36%)
  local copies, waits for them, and re-layouts  122 us (21%)
  blocking collectives  76.2 us (13%)
  starting transfers between devices  65.7 us (11%)
  matrix products  63.9 us (11%)
  other arithmetic  31.3 us (5%)
  between operations  15.4 us (3%)
    all_to_all x1, waiting for transfers between devices, local(): lax.all_to_all(zxo_rows, 'mp', split_axis=2, concat_axis=3, tiled=True)[0]  102 us
    all_to_all x5, blocking collectives, copy_for_each(): lax.all_to_all(jnp.broadcast_to(array[None], (devices, *array.shape)), ax...  62.5 us
    all_to_all x11, waiting for transfers between devices, copy_for_each(): lax.all_to_all(jnp.broadcast_to(array[None], (devices, *array.shape)), ax...  48.7 us
    all_to_all x11, starting transfers between devices, copy_for_each(): lax.all_to_all(jnp.broadcast_to(array[None], (devices, *array.shape)), ax...  48 us
    unnamed x157, local copies, waits for them, and re-layouts  42.3 us
    dot_general x21, matrix products, project(): lax.dot_general(inputs, weights, (((1,), (1,)), ((), ())), preferred_elem...  33 us
    ppermute x6, waiting for transfers between devices, passed_along(): return lax.ppermute(array, axis, pairs)  30.1 us
    all_gather x1, waiting for transfers between devices, local(): lax.all_gather(w_zxo, 'dp', axis=2, tiled=True)  29.2 us
  transfers between devices with their start and end apart: 19, of which 16 were waited for; matrix products, arithmetic and copies ran while one was open for 17% of the time, Pallas kernels for 0%

commit v1 on v0

v1 whole, which is shorter than its diff:
```python
import functools

import jax
import jax.numpy as jnp
from jax import lax
from jax.experimental import pallas as pl
from jax.experimental.pallas import tpu as pltpu
from jax.sharding import PartitionSpec as P

EPS = 1e-05
F32 = jnp.float32
BF16 = jnp.bfloat16
LANES = 128


def silu(v):
    return v * (1.0 / (1.0 + jnp.exp(-v)))


def softplus(v):
    return jnp.maximum(v, 0.0) + jnp.log1p(jnp.exp(-jnp.abs(v)))


def halves(v):
    top = v.astype(BF16).astype(F32)
    return top, v - top


def iota(shape, dim):
    return lax.broadcasted_iota(jnp.int32, shape, dim)


def mm(a, b):
    return lax.dot_general(a, b, (((1,), (0,)), ((), ())), preferred_element_type=F32)


def mm_t(a, b):
    return lax.dot_general(a, b, (((1,), (1,)), ((), ())), preferred_element_type=F32)


def kernel(
    size,
    len_s,
    slot_s,
    rate_s,
    bias_s,
    skip_s,
    hid_h,
    gain_h,
    w_h,
    wb_h,
    cxw_h,
    cbw_h,
    cxp_h,
    cbp_h,
    st_h,
    gg_h,
    hid_o,
    st_o,
    hid,
    gain,
    w,
    wb,
    cxw,
    cbw,
    cxp,
    cbp,
    st,
    gg,
    wg,
    perm,
    wsmall,
    h,
    past_x,
    past_b,
    alive,
    expand,
    old16,
    wide_b,
    wide_c,
    outer_l,
    outer_t,
    new,
    hid_new,
    send_s,
    send_m,
    send_b,
    send_c,
    recv_x,
    recv_s,
    recv_m,
    recv_b,
    recv_c,
    recv_h,
    recv_o,
    load_sem,
    store_sem,
    out_sem,
    send_sem,
    x_sem,
    w_sem,
    s_sem,
    m_sem,
    b_sem,
    c_sem,
    h_sem,
    o_sem,
):
    nd, nm, ns, rows, feat, chan, head, small, bcw, slots_dev, width, inner = size
    ratio = nm // nd
    pairs = ratio // 2
    d = lax.axis_index("dp")
    m = lax.axis_index("mp")
    sec = lax.axis_index("section")
    home = m // ratio
    mine = lax.rem(m, ratio)
    odd = lax.rem(mine, 2) == 1
    on_home = home == d
    per_dp = small // nd
    all_rows = nd * rows
    heads_dev = chan // head
    first = sec == 0
    last = sec == ns - 1

    srcs = (
        (hid_h, hid),
        (gain_h, gain),
        (wb_h, wb),
        (w_h, w),
        (cxw_h, cxw),
        (cbw_h, cbw),
        (cxp_h, cxp),
        (cbp_h, cbp),
        (st_h, st),
        (gg_h, gg),
    )
    loads = [
        pltpu.make_async_copy(src, dst, load_sem.at[i]) for i, (src, dst) in enumerate(srcs)
    ]
    for copy in loads:
        copy.start()

    barrier = pltpu.get_barrier_semaphore()

    def tell(dp, mp, section=None):
        where = {"dp": dp, "mp": mp}
        if section is not None:
            where["section"] = section
        pl.semaphore_signal(
            barrier, inc=1, device_id=where, device_id_type=pl.DeviceIdType.MESH
        )

    for i in range(nm):

        @pl.when(jnp.logical_not(on_home & (m == i)))
        def _():
            tell(home, i)

    for i in range(nd):
        for j in range(ratio):

            @pl.when(jnp.logical_not((d == i) & (m == d * ratio + j)))
            def _():
                tell(i, d * ratio + j)

    for k in range(1, nd):
        tell(lax.rem(d + k, nd), m)

    @pl.when(sec > 0)
    def _():
        for k in range(nd):
            tell(k, m, sec - 1)

    own = jnp.where(on_home, 1, 0)
    pl.semaphore_wait(
        barrier, 2 * (nm - own) + nd - 1 + jnp.where(sec < ns - 1, nd, 0)
    )

    sent = []

    def send(src, dst, recv, where, self_too=None, only=None):
        sem = send_sem.at[len(sent)]
        copy = pltpu.make_async_remote_copy(
            src_ref=src,
            dst_ref=dst,
            send_sem=sem,
            recv_sem=recv,
            device_id=where,
            device_id_type=pl.DeviceIdType.MESH,
        )
        if only is not None:

            @pl.when(only)
            def _():
                copy.start()

            sent.append((copy, only))
        elif self_too is None:
            copy.start()
            sent.append((copy, None))
        else:

            @pl.when(jnp.logical_not(self_too))
            def _():
                copy.start()

            @pl.when(self_too)
            def _():
                pltpu.make_async_copy(src, dst, recv).start()

            sent.append((copy, jnp.logical_not(self_too)))

    def arrived(ref, sem):
        pltpu.make_async_copy(ref, ref, sem).wait()

    loads[0].wait()
    loads[2].wait()
    group_w = wg.shape[2]
    wg[d] = jnp.zeros((feat, group_w), BF16)
    wg[d, :, 0:per_dp] = wb[...]
    my_rows = pl.ds(pl.multiple_of(d * rows, rows), rows)
    for k in range(1, nd):
        there = {"dp": lax.rem(d + k, nd), "mp": m}
        send(wg.at[d], wg.at[d], w_sem.at[d], there)
    for k in range(1, nd):
        there = {"dp": lax.rem(d + k, nd), "mp": m}
        send(hid, recv_x.at[my_rows], x_sem.at[d], there)
    recv_x[my_rows, :] = hid[...]

    col = iota(perm.shape, 1)
    row = iota(perm.shape, 0)
    group = row // group_w
    inside = row - group * group_w
    perm[...] = jnp.where(
        (inside < per_dp) & (col == group * per_dp + inside), 1.0, 0.0
    ).astype(BF16)
    lane_of = iota((LANES, chan), 1) // head
    expand[...] = jnp.where(
        iota((LANES, chan), 0) == m * heads_dev + lane_of, 1.0, 0.0
    ).astype(BF16)
    wide_b[...] = jnp.zeros_like(wide_b)
    wide_c[...] = jnp.zeros_like(wide_c)
    outer_l[...] = jnp.zeros_like(outer_l)
    loads[1].wait()
    offset = m * feat
    base = offset // LANES
    gain_w = gain[:, pl.ds(pl.multiple_of(base * LANES, LANES), 2 * LANES)]
    gain_w = jnp.broadcast_to(gain_w, (8, 2 * LANES))
    gain_w = pltpu.roll(
        gain_w, lax.rem(2 * LANES - (offset - base * LANES), 2 * LANES), 1
    )
    gain_row = gain_w[0:1, 0:feat]

    for k in range(1, nd):
        i = lax.rem(d + k, nd)
        arrived(wg.at[i], w_sem.at[i])
    total = mm(wg[0], perm[0:group_w, :])
    for i in range(1, nd):
        total += mm(wg[i], perm[i * group_w : (i + 1) * group_w, :])
    wsmall[...] = total.astype(BF16)
    for k in range(1, nd):
        i = lax.rem(d + k, nd)
        block = pl.ds(pl.multiple_of(i * rows, rows), rows)
        arrived(recv_x.at[block], x_sem.at[i])

    def prepare():
        for copy in loads[4:9]:
            copy.wait()
        tap = iota((3, 1), 0)
        taps_x = cxw[0:3, :]
        taps_b = cbw[0:3, :]

        def one(s, carry):
            slot = jnp.clip(slot_s[s] - d * slots_dev, 0, slots_dev - 1)
            seen = (tap + len_s[s] >= 3).astype(F32)
            past_x[pl.ds(s, 1), :] = jnp.sum(
                cxp[slot].astype(F32) * seen * taps_x, axis=0, keepdims=True
            )
            past_b[pl.ds(s, 1), :] = jnp.sum(
                cbp[slot].astype(F32) * seen * taps_b, axis=0, keepdims=True
            )
            alive[pl.ds(s, 1), :] = jnp.full(
                (1, LANES), jnp.where(len_s[s] > 0, 1.0, 0.0), F32
            )
            old16[s] = st[slot].astype(BF16)
            return carry

        lax.fori_loop(0, rows, one, 0)

    @pl.when(first)
    def _():
        h[...] = recv_x[...]

    @pl.when(jnp.logical_not(first))
    def _():
        prepare()
        arrived(recv_h, h_sem.at[0])
        acc = None
        for i in range(nd):
            arrived(recv_c.at[i], c_sem.at[i])
            part = recv_c[i].astype(F32)
            acc = part if acc is None else acc + part
        lane = iota(acc.shape, 1)
        squares = jnp.sum(
            jnp.where((lane == feat) | (lane == feat + 1), acc, 0.0), axis=1, keepdims=True
        )
        scale = lax.rsqrt(squares / inner + EPS)
        h[...] = (recv_h[...].astype(F32) + acc[:, 0:feat] * scale).astype(BF16)

    value = h[...].astype(F32)
    squares = jnp.sum(value * value, axis=1, keepdims=True)
    v = (value * gain_row).astype(BF16)
    out = mm(v, wsmall[...])
    high, low = halves(squares)
    lane = iota(out.shape, 1)
    out = jnp.where(lane == small, high, jnp.where(lane == small + 1, low, out))
    send_s[...] = out.astype(BF16)
    for k in range(nd):
        i = lax.rem(d + k, nd)
        block = pl.ds(pl.multiple_of(i * rows, rows), rows)
        for j in range(ratio):
            there = {"dp": i, "mp": d * ratio + j}
            send(
                send_s.at[block],
                recv_s.at[m],
                s_sem.at[m],
                there,
                (i == d) & (m == d * ratio + j),
            )
    loads[3].wait()
    pair = 2 * chan
    window = 3 * LANES
    for p in range(pairs):
        cols = slice(p * pair, (p + 1) * pair)
        send_m[0, :, cols] = mm(v, w[1, :, cols]).astype(BF16)
        send_m[1, :, cols] = mm(v, w[0, :, cols]).astype(BF16)
        for k in range(nd):
            i = lax.rem(d + k, nd)
            block = pl.ds(pl.multiple_of(i * rows, rows), rows)
            for e in range(2):
                j = 2 * p + e
                start = p * pair + e * (pair - window)
                there = {"dp": i, "mp": d * ratio + j}
                send(
                    send_m.at[:, block, start : start + window],
                    recv_m.at[m],
                    m_sem.at[m],
                    there,
                    (i == d) & (m == d * ratio + j),
                )

    more = jnp.logical_not(last)
    after = jnp.minimum(sec + 1, ns - 1)
    send(h, recv_h, h_sem.at[0], {"dp": d, "mp": m, "section": after}, only=more)

    @pl.when(first)
    def _():
        prepare()

    loads[9].wait()
    per_head = iota((1, chan), 1) // head
    rate_row = jnp.zeros((1, chan), F32)
    bias_row = jnp.zeros((1, chan), F32)
    skip_row = jnp.zeros((1, chan), F32)
    for i in range(heads_dev):
        rate_row = jnp.where(per_head == i, rate_s[0, i], rate_row)
        bias_row = jnp.where(per_head == i, bias_s[0, i], bias_row)
        skip_row = jnp.where(per_head == i, skip_s[0, i], skip_row)

    acc = None
    for i in range(nm):
        arrived(recv_s.at[i], s_sem.at[i])
        part = recv_s[i].astype(F32)
        acc = part if acc is None else acc + part
    lane = iota(acc.shape, 1)
    squares = jnp.sum(
        jnp.where((lane == small) | (lane == small + 1), acc, 0.0), axis=1, keepdims=True
    )
    scale = lax.rsqrt(squares / width + EPS)
    conv_b = silu(past_b[...] + acc[:, 0:bcw] * scale * cbw[3:4, :])
    b_cur = conv_b[:, 0 : bcw // 2]
    c_cur = conv_b[:, bcw // 2 :]
    high, low = halves(acc[:, bcw:])
    raw = mm(high.astype(BF16), expand[...]) + mm(low.astype(BF16), expand[...])
    step = softplus(raw * scale + bias_row)
    decay = jnp.exp(-step * rate_row) * alive[:, 0:1]
    c_high, c_low = halves(c_cur)
    c_two = jnp.concatenate([c_high, c_low], axis=0).astype(BF16)
    c_row = lax.rem(iota((2 * rows, 1), 0), rows)

    def ask(s, carry):
        return carry + mm_t(jnp.where(c_row == s, c_two, jnp.zeros_like(c_two)), old16[s])

    both = lax.fori_loop(0, rows, ask, jnp.zeros((2 * rows, chan), F32), unroll=4)
    read = both[0:rows] + both[rows:]
    bc_dot = jnp.sum(b_cur * c_cur, axis=1, keepdims=True)

    acc = None
    for i in range(nm):
        arrived(recv_m.at[i], m_sem.at[i])
        part = recv_m[i].astype(F32)
        acc = part if acc is None else acc + part
    acc_i, acc_g = acc[0], acc[1]
    acc_i = jnp.where(odd, pltpu.roll(acc_i, chan, 1), acc_i)[:, 0:chan]
    acc_g = jnp.where(odd, pltpu.roll(acc_g, chan, 1), acc_g)[:, 0:chan]
    x = silu(past_x[...] + acc_i * scale * cxw[3:4, :])
    sx = step * x
    gated = (decay * read + sx * bc_dot + skip_row * x) * silu(acc_g * scale)
    squares = jnp.sum(gated * gated, axis=1, keepdims=True)
    wide_b[:, 0:chan] = gated * gg[...]
    full = wide_b[...]
    high, low = halves(squares)
    lane = iota(full.shape, 1)
    full = jnp.where(lane == chan, high, jnp.where(lane == chan + 1, low, full))
    full = jnp.where(odd, pltpu.roll(full, window - chan, 1), full)
    send_b[...] = full.astype(BF16)
    for k in range(nm):
        i = lax.rem(m + k, nm)
        there = {"dp": home, "mp": i}
        send(
            send_b,
            recv_b.at[mine, my_rows],
            b_sem.at[mine * nd + d],
            there,
            on_home & (m == i),
        )

    s_high, s_low = halves(sx)
    d_high, d_low = halves(decay)
    b_high, b_low = halves(b_cur)
    outer_l[0:rows, 0:chan] = s_high
    outer_l[rows : 2 * rows, 0:chan] = s_high
    outer_l[2 * rows : 3 * rows, 0:chan] = s_low
    outer_l[3 * rows : 4 * rows, 0:chan] = d_high
    outer_l[4 * rows : 5 * rows, 0:chan] = d_low
    outer_t[...] = jnp.transpose(outer_l[...])[0:chan, :].astype(BF16)
    zero = jnp.zeros((rows, LANES), F32)
    one_ = jnp.ones((rows, LANES), F32)
    right = jnp.concatenate(
        [
            jnp.concatenate([b_high, b_low, b_high, zero, zero], axis=0),
            jnp.concatenate([zero, zero, zero, one_, one_], axis=0),
        ],
        axis=1,
    )
    right = jnp.concatenate(
        [right, jnp.zeros((LANES - 5 * rows, 2 * LANES), F32)], axis=0
    ).astype(BF16)
    r_row = lax.rem(iota((LANES, 1), 0), rows)

    def update(s, carry):
        slot = jnp.clip(slot_s[s] - d * slots_dev, 0, slots_dev - 1)
        both = mm(outer_t[...], jnp.where(r_row == s, right, jnp.zeros_like(right)))
        new[s] = both[:, LANES:] * st[slot] + both[:, 0:LANES]
        pltpu.make_async_copy(new.at[s], st_o.at[s], store_sem.at[s]).start()
        return carry

    lax.fori_loop(0, rows // 2, update, 0)

    out = jnp.zeros((all_rows, feat), F32)
    squares = jnp.zeros((all_rows, 1), F32)
    lane = iota((all_rows, LANES), 1)
    for p in range(pairs):
        for e in range(2):
            for i in range(nd):
                arrived(
                    recv_b.at[2 * p + e, i * rows : (i + 1) * rows],
                    b_sem.at[(2 * p + e) * nd + i],
                )
        even_t = recv_b[2 * p, :, 2 * LANES : 3 * LANES].astype(F32)
        odd_t = recv_b[2 * p + 1, :, 0:LANES].astype(F32)
        gap = chan - 2 * LANES
        squares += jnp.sum(
            jnp.where((lane == gap) | (lane == gap + 1), even_t, 0.0)
            + jnp.where(lane < 2, odd_t, 0.0),
            axis=1,
            keepdims=True,
        )
        middle = jnp.where(lane < gap, even_t, odd_t).astype(BF16)
        at = p * pair
        out += mm_t(recv_b[2 * p, :, 0 : 2 * LANES], w[2, :, at : at + 2 * LANES])
        out += mm_t(middle, w[2, :, at + 2 * LANES : at + 3 * LANES])
        out += mm_t(recv_b[2 * p + 1, :, LANES:window], w[2, :, at + 3 * LANES : at + pair])
    wide_c[:, 0:feat] = out
    full = wide_c[...]
    high, low = halves(squares)
    lane = iota(full.shape, 1)
    full = jnp.where(lane == feat, high, jnp.where(lane == feat + 1, low, full))
    send_c[...] = full.astype(BF16)

    for k in range(nd):
        there = {"dp": lax.rem(d + k, nd), "mp": m, "section": after}
        send(send_c, recv_c.at[d], c_sem.at[d], there, only=more)
    for k in range(1, nd):
        i = lax.rem(d + k, nd)
        block = pl.ds(pl.multiple_of(i * rows, rows), rows)
        send(send_c.at[block], recv_o.at[d], o_sem.at[d], {"dp": i, "mp": m})
    recv_o[d] = send_c[my_rows, :]

    lax.fori_loop(rows // 2, rows, update, 0)

    for k in range(1, nd):
        i = lax.rem(d + k, nd)
        arrived(recv_o.at[i], o_sem.at[i])
    acc = recv_o[0].astype(F32)
    for i in range(1, nd):
        acc += recv_o[i].astype(F32)
    lane = iota(acc.shape, 1)
    squares = jnp.sum(
        jnp.where((lane == feat) | (lane == feat + 1), acc, 0.0), axis=1, keepdims=True
    )
    scale = lax.rsqrt(squares / inner + EPS)
    hid_new[...] = (h[my_rows, :].astype(F32) + acc[:, 0:feat] * scale).astype(BF16)
    result = pltpu.make_async_copy(hid_new, hid_o, out_sem.at[0])
    result.start()

    for copy, cond in sent:
        if cond is None:
            copy.wait_send()
        else:

            @pl.when(cond)
            def _():
                copy.wait_send()

    def drain(s, carry):
        pltpu.make_async_copy(new.at[s], st_o.at[s], store_sem.at[s]).wait()
        return carry

    lax.fori_loop(0, rows, drain, 0)
    result.wait()


def local(
    hidden_in,
    lengths,
    slots,
    norm_gain,
    w_zxo,
    w_bcdt,
    conv_x_weight,
    conv_bc_weight,
    conv_x_pool,
    conv_bc_pool,
    state_pool,
    a_rate,
    dt_bias,
    skip_gain,
    gate_gain,
):
    nd, nm, ns = (lax.axis_size(name) for name in ("dp", "mp", "section"))
    rows, feat = hidden_in.shape
    width = norm_gain.shape[1]
    chan_dp = w_zxo.shape[2]
    per_dp = w_bcdt.shape[1]
    slots_dev, heads_dev, head, state = state_pool.shape[1:]
    chan = heads_dev * head
    bcw = conv_bc_weight.shape[2]
    small = per_dp * nd
    small_pad = -(-(small + 2) // LANES) * LANES
    group_w = -(-per_dp // LANES) * LANES
    ratio = nm // nd
    all_rows = nd * rows
    window = 3 * LANES
    size = (
        nd, nm, ns, rows, feat, chan, head, small, bcw, slots_dev, width, chan * nm,
    )
    operands = (
        lengths,
        slots,
        a_rate,
        dt_bias,
        skip_gain,
        hidden_in,
        norm_gain,
        jnp.swapaxes(w_zxo[0], 1, 2),
        jnp.swapaxes(w_bcdt[0], 0, 1),
        conv_x_weight[0],
        conv_bc_weight[0],
        conv_x_pool[0],
        conv_bc_pool[0],
        state_pool.reshape(slots_dev, chan, state),
        gate_gain,
    )
    sends = 2 * (nd - 1) + 2 * nd * ratio + nm + 2 * nd
    dma = pltpu.SemaphoreType.DMA
    scratch = (
        [pltpu.VMEM(a.shape, a.dtype) for a in operands[5:]]
        + [
            pltpu.VMEM((nd, feat, group_w), BF16),
            pltpu.VMEM((nd * group_w, small_pad), BF16),
            pltpu.VMEM((feat, small_pad), BF16),
            pltpu.VMEM((all_rows, feat), BF16),
            pltpu.VMEM((rows, chan), F32),
            pltpu.VMEM((rows, bcw), F32),
            pltpu.VMEM((rows, LANES), F32),
            pltpu.VMEM((LANES, chan), BF16),
            pltpu.VMEM((rows, chan, state), BF16),
            pltpu.VMEM((rows, window), F32),
            pltpu.VMEM((all_rows, 2 * LANES), F32),
            pltpu.VMEM((LANES, window), F32),
            pltpu.VMEM((chan, LANES), BF16),
            pltpu.VMEM((rows, chan, state), F32),
            pltpu.VMEM((rows, feat), BF16),
        ]
        + [
            pltpu.VMEM((all_rows, small_pad), BF16),
            pltpu.VMEM((2, all_rows, chan_dp), BF16),
            pltpu.VMEM((rows, window), BF16),
            pltpu.VMEM((all_rows, 2 * LANES), BF16),
        ]
        + [
            pltpu.VMEM((all_rows, feat), BF16),
            pltpu.VMEM((nm, rows, small_pad), BF16),
            pltpu.VMEM((nm, 2, rows, window), BF16),
            pltpu.VMEM((ratio, all_rows, window), BF16),
            pltpu.VMEM((nd, all_rows, 2 * LANES), BF16),
            pltpu.VMEM((all_rows, feat), BF16),
            pltpu.VMEM((nd, rows, 2 * LANES), BF16),
        ]
        + [
            dma((10,)),
            dma((rows,)),
            dma((1,)),
            dma((sends,)),
            dma((nd,)),
            dma((nd,)),
            dma((nm,)),
            dma((nm,)),
            dma((nd * ratio,)),
            dma((nd,)),
            dma((1,)),
            dma((nd,)),
        ]
    )
    hidden, states = pl.pallas_call(
        functools.partial(kernel, size),
        out_shape=(
            jax.ShapeDtypeStruct((rows, feat), BF16),
            jax.ShapeDtypeStruct((rows, chan, state), F32),
        ),
        in_specs=[pl.BlockSpec(memory_space=pltpu.SMEM)] * 5
        + [pl.BlockSpec(memory_space=pl.ANY)] * 10,
        out_specs=(
            pl.BlockSpec(memory_space=pl.ANY),
            pl.BlockSpec(memory_space=pl.ANY),
        ),
        scratch_shapes=scratch,
        compiler_params=pltpu.CompilerParams(
            collective_id=0, has_side_effects=True, vmem_limit_bytes=48 << 20
        ),
    )(*operands)
    return (
        hidden[None],
        states.reshape(1, rows, heads_dev, head, state),
    )


def solution(mesh):
    placed = (
        P("dp", "mp"),
        P("dp"),
        P("dp"),
        P("section", None),
        P("section", None, "dp", "mp"),
        P("section", "dp", "mp"),
        P("section", None, "mp"),
        P("section", None, None),
        P("section", "dp", None, "mp"),
        P("section", "dp", None, None),
        P("section", "dp", "mp", None, None),
        P("section", "mp"),
        P("section", "mp"),
        P("section", "mp"),
        P("section", "mp"),
    )
    return jax.shard_map(
        local,
        mesh=mesh,
        in_specs=placed,
        out_specs=(P("section", "dp", "mp"), P("section", "dp", "mp", None, None)),
        check_vma=False,
    )
```

time: 590 us -> 136 us (0.23)
  the two profiles are of different devices: /device:TPU:128 before, /device:TPU:129 now
where the time goes in v1:
time: 136 us; the launch traced here: 135 us
  Pallas kernels  122 us (90%)
  local copies, waits for them, and re-layouts  12.5 us (9%)
    pallas_call x1, Pallas kernels, local(): pl.pallas_call(functools.partial(kernel, size), out_shape=(jax.ShapeDtype...  122 us
    unnamed x30, local copies, waits for them, and re-layouts  12.5 us

profile of v1, /device:TPU:129, one launch (start us, length us, event | category | flops | bytes accessed | tf_op | source)
XLA Modules:
  0.0 134.9 jit_solution(9165362475275125670)
XLA Ops:
  0.6 0.0 copy-start
  0.6 1.3 copy-done
  1.9 0.0 copy-start.1
  1.9 0.8 copy-done.1
  2.7 0.0 copy-start.2
  2.7 0.8 copy-done.2
  3.5 0.0 copy-start.3
  3.5 0.8 copy-done.3
  4.3 0.0 copy-start.4
  4.3 0.7 copy-done.4
  5.0 0.0 copy-start.5
  5.0 0.7 copy-done.5
  5.7 0.0 copy-start.6
  5.7 0.7 copy-done.6
  6.4 0.0 copy-start.7
  6.4 0.7 copy-done.7
  7.1 0.0 copy-start.8
  7.1 0.7 copy-done.8
  7.7 0.0 copy-start.9
  7.7 0.7 copy-done.9
  8.4 0.0 copy-start.10
  8.4 0.7 copy-done.10
  9.1 0.0 copy-start.11
  9.1 0.7 copy-done.11
  9.7 0.0 copy-start.12
  9.7 0.7 copy-done.12
  10.4 0.0 copy-start.13
  10.4 0.7 copy-done.13
  11.0 121.7 %shard_map.158 = (bf16[16,160]{1,0:T(8,128)(2,1)S(1)}, f32[16,320,128]{2,1,0:T(8,128)S(1)}) custom-call(s32[16]{0:T(128)S(1)} %copy-done.9, s32[16]{0:T(128)S(1)} %copy-done.10, f32[1,5]{1,0:T(1,128)S(1)} %copy-done.11, f32[1,5]{1,0:T(1,128)S(1)} %copy-done.12, f32[1,5]{1,0:T(1,128)S(1)} %copy-done.13, bf16[16,160]{1,0:T(8,128)(2,1)S(1)} %copy-done.5, ...), custom_call_target="tpu_custom_call" | custom-call | tf_op jit(solution)/shard_map/pallas_call | solution.py:636
  132.8 0.6 copy.19
  133.4 1.5 %copy.20 = f32[1,16,5,64,128]{4,3,2,1,0:T(8,128)} copy(f32[1,16,5,64,128]{4,3,2,1,0:T(8,128)S(1)} %bitcast.13) | data formatting | bytes 5242880
Async XLA Ops:
  0.6 1.3 copy-start
  1.9 0.8 copy-start.1
  2.7 0.8 copy-start.2
  3.5 0.8 copy-start.3
  4.3 0.7 copy-start.4
  5.0 0.7 copy-start.5
  5.7 0.7 copy-start.6
  6.4 0.7 copy-start.7
  7.1 0.7 copy-start.8
  7.7 0.7 copy-start.9
  8.4 0.7 copy-start.10
  9.1 0.7 copy-start.11
  9.7 0.7 copy-start.12
  10.4 0.7 copy-start.13

commit v2 on v1

--- a/solution.py
+++ b/solution.py
@@ -40,11 +40,11 @@
 
 def kernel(
     size,
-    len_s,
-    slot_s,
-    rate_s,
-    bias_s,
-    skip_s,
+    len_h,
+    slot_h,
+    rate_h,
+    bias_h,
+    skip_h,
     hid_h,
     gain_h,
     w_h,
@@ -57,6 +57,11 @@
     gg_h,
     hid_o,
     st_o,
+    len_s,
+    slot_s,
+    rate_s,
+    bias_s,
+    skip_s,
     hid,
     gain,
     w,
@@ -133,6 +138,11 @@
         (cbp_h, cbp),
         (st_h, st),
         (gg_h, gg),
+        (len_h, len_s),
+        (slot_h, slot_s),
+        (rate_h, rate_s),
+        (bias_h, bias_s),
+        (skip_h, skip_s),
     )
     loads = [
         pltpu.make_async_copy(src, dst, load_sem.at[i]) for i, (src, dst) in enumerate(srcs)
@@ -165,6 +175,8 @@
 
     for k in range(1, nd):
         tell(lax.rem(d + k, nd), m)
+    for k in range(1, nm):
+        tell(d, lax.rem(m + k, nm))
 
     @pl.when(sec > 0)
     def _():
@@ -173,7 +185,7 @@
 
     own = jnp.where(on_home, 1, 0)
     pl.semaphore_wait(
-        barrier, 2 * (nm - own) + nd - 1 + jnp.where(sec < ns - 1, nd, 0)
+        barrier, 2 * (nm - own) + nd - 1 + nm - 1 + jnp.where(sec < ns - 1, nd, 0)
     )
 
     sent = []
@@ -264,7 +276,7 @@
         arrived(recv_x.at[block], x_sem.at[i])
 
     def prepare():
-        for copy in loads[4:9]:
+        for copy in loads[4:9] + loads[10:]:
             copy.wait()
         tap = iota((3, 1), 0)
         taps_x = cxw[0:3, :]
@@ -307,42 +319,45 @@
         scale = lax.rsqrt(squares / inner + EPS)
         h[...] = (recv_h[...].astype(F32) + acc[:, 0:feat] * scale).astype(BF16)
 
-    value = h[...].astype(F32)
+    value = h[my_rows, :].astype(F32)
     squares = jnp.sum(value * value, axis=1, keepdims=True)
-    v = (value * gain_row).astype(BF16)
-    out = mm(v, wsmall[...])
+    out = mm((value * gain_row).astype(BF16), wsmall[...])
     high, low = halves(squares)
     lane = iota(out.shape, 1)
     out = jnp.where(lane == small, high, jnp.where(lane == small + 1, low, out))
     send_s[...] = out.astype(BF16)
-    for k in range(nd):
-        i = lax.rem(d + k, nd)
-        block = pl.ds(pl.multiple_of(i * rows, rows), rows)
-        for j in range(ratio):
-            there = {"dp": i, "mp": d * ratio + j}
-            send(
-                send_s.at[block],
-                recv_s.at[m],
-                s_sem.at[m],
-                there,
-                (i == d) & (m == d * ratio + j),
-            )
+    for k in range(1, nm):
+        there = {"dp": d, "mp": lax.rem(m + k, nm)}
+        send(send_s, recv_s.at[m], s_sem.at[m], there)
+    recv_s[m] = send_s[...]
+    v = (h[...].astype(F32) * gain_row).astype(BF16)
     loads[3].wait()
     pair = 2 * chan
+    two = 2 * LANES
+    gap = chan - two
     window = 3 * LANES
+    lane = iota((all_rows, LANES), 1)
     for p in range(pairs):
-        cols = slice(p * pair, (p + 1) * pair)
-        send_m[0, :, cols] = mm(v, w[1, :, cols]).astype(BF16)
-        send_m[1, :, cols] = mm(v, w[0, :, cols]).astype(BF16)
-        for k in range(nd):
+        at = p * pair
+        cols = slice(at, at + pair)
+        inner_p = mm(v, w[1, :, cols])
+        gate_p = mm(v, w[0, :, cols])
+        inner_t = inner_p[:, two:window]
+        gate_t = pltpu.roll(gate_p[:, two:window], gap, 1)
+        send_m[2 * p, :, 0:two] = inner_p[:, 0:two].astype(BF16)
+        send_m[2 * p, :, two : 2 * two] = gate_p[:, 0:two].astype(BF16)
+        send_m[2 * p, :, 2 * two :] = jnp.where(lane < gap, inner_t, gate_t).astype(BF16)
+        send_m[2 * p + 1, :, 0:two] = inner_p[:, window:].astype(BF16)
+        send_m[2 * p + 1, :, two : 2 * two] = gate_p[:, window:].astype(BF16)
+        send_m[2 * p + 1, :, 2 * two :] = jnp.where(lane < gap, gate_t, inner_t).astype(BF16)
+        for k in (2, 1, 3, 0) if nd == 4 else range(nd):
             i = lax.rem(d + k, nd)
             block = pl.ds(pl.multiple_of(i * rows, rows), rows)
             for e in range(2):
                 j = 2 * p + e
-                start = p * pair + e * (pair - window)
                 there = {"dp": i, "mp": d * ratio + j}
                 send(
-                    send_m.at[:, block, start : start + window],
+                    send_m.at[j, block],
                     recv_m.at[m],
                     m_sem.at[m],
                     there,
@@ -368,8 +383,10 @@
         skip_row = jnp.where(per_head == i, skip_s[0, i], skip_row)
 
     acc = None
-    for i in range(nm):
-        arrived(recv_s.at[i], s_sem.at[i])
+    for k in range(nm):
+        i = lax.rem(m + k, nm)
+        if k > 0:
+            arrived(recv_s.at[i], s_sem.at[i])
         part = recv_s[i].astype(F32)
         acc = part if acc is None else acc + part
     lane = iota(acc.shape, 1)
@@ -400,9 +417,16 @@
         arrived(recv_m.at[i], m_sem.at[i])
         part = recv_m[i].astype(F32)
         acc = part if acc is None else acc + part
-    acc_i, acc_g = acc[0], acc[1]
-    acc_i = jnp.where(odd, pltpu.roll(acc_i, chan, 1), acc_i)[:, 0:chan]
-    acc_g = jnp.where(odd, pltpu.roll(acc_g, chan, 1), acc_g)[:, 0:chan]
+    tile = acc[:, 2 * two :]
+    other = pltpu.roll(tile, gap, 1)
+
+    def in_order(part, edge):
+        before = jnp.concatenate([edge, part], axis=1)
+        after = jnp.concatenate([part, edge], axis=1)
+        return jnp.where(odd, pltpu.roll(before, chan, 1), after)[:, 0:chan]
+
+    acc_i = in_order(acc[:, 0:two], tile)
+    acc_g = in_order(acc[:, two : 2 * two], other)
     x = silu(past_x[...] + acc_i * scale * cxw[3:4, :])
     sx = step * x
     gated = (decay * read + sx * bc_dot + skip_row * x) * silu(acc_g * scale)
@@ -469,7 +493,6 @@
                 )
         even_t = recv_b[2 * p, :, 2 * LANES : 3 * LANES].astype(F32)
         odd_t = recv_b[2 * p + 1, :, 0:LANES].astype(F32)
-        gap = chan - 2 * LANES
         squares += jnp.sum(
             jnp.where((lane == gap) | (lane == gap + 1), even_t, 0.0)
             + jnp.where(lane < 2, odd_t, 0.0),
@@ -582,10 +605,11 @@
         state_pool.reshape(slots_dev, chan, state),
         gate_gain,
     )
-    sends = 2 * (nd - 1) + 2 * nd * ratio + nm + 2 * nd
+    sends = 2 * (nd - 1) + nd * ratio + 2 * nm - 1 + 2 * nd
     dma = pltpu.SemaphoreType.DMA
     scratch = (
-        [pltpu.VMEM(a.shape, a.dtype) for a in operands[5:]]
+        [pltpu.SMEM(a.shape, a.dtype) for a in operands[:5]]
+        + [pltpu.VMEM(a.shape, a.dtype) for a in operands[5:]]
         + [
             pltpu.VMEM((nd, feat, group_w), BF16),
             pltpu.VMEM((nd * group_w, small_pad), BF16),
@@ -604,22 +628,22 @@
             pltpu.VMEM((rows, feat), BF16),
         ]
         + [
-            pltpu.VMEM((all_rows, small_pad), BF16),
-            pltpu.VMEM((2, all_rows, chan_dp), BF16),
+            pltpu.VMEM((rows, small_pad), BF16),
+            pltpu.VMEM((ratio, all_rows, 2 * chan), BF16),
             pltpu.VMEM((rows, window), BF16),
             pltpu.VMEM((all_rows, 2 * LANES), BF16),
         ]
         + [
             pltpu.VMEM((all_rows, feat), BF16),
             pltpu.VMEM((nm, rows, small_pad), BF16),
-            pltpu.VMEM((nm, 2, rows, window), BF16),
+            pltpu.VMEM((nm, rows, 2 * chan), BF16),
             pltpu.VMEM((ratio, all_rows, window), BF16),
             pltpu.VMEM((nd, all_rows, 2 * LANES), BF16),
             pltpu.VMEM((all_rows, feat), BF16),
             pltpu.VMEM((nd, rows, 2 * LANES), BF16),
         ]
         + [
-            dma((10,)),
+            dma((15,)),
             dma((rows,)),
             dma((1,)),
             dma((sends,)),
@@ -639,8 +663,8 @@
             jax.ShapeDtypeStruct((rows, feat), BF16),
             jax.ShapeDtypeStruct((rows, chan, state), F32),
         ),
-        in_specs=[pl.BlockSpec(memory_space=pltpu.SMEM)] * 5
-        + [pl.BlockSpec(memory_space=pl.ANY)] * 10,
+        in_specs=[pl.BlockSpec(memory_space=pltpu.HBM)] * 5
+        + [pl.BlockSpec(memory_space=pltpu.HBM)] * 10,
         out_specs=(
             pl.BlockSpec(memory_space=pl.ANY),
             pl.BlockSpec(memory_space=pl.ANY),
@@ -649,7 +673,7 @@
         compiler_params=pltpu.CompilerParams(
             collective_id=0, has_side_effects=True, vmem_limit_bytes=48 << 20
         ),
-    )(*operands)
+    )(*[pltpu.with_memory_space_constraint(a, pltpu.HBM) for a in operands])
     return (
         hidden[None],
         states.reshape(1, rows, heads_dev, head, state),

time: 136 us -> 103 us (0.76); the launches traced: 135 us -> 103 us
  Pallas kernels: 122 us -> 101 us
  local copies, waits for them, and re-layouts: 12.5 us -> 2.09 us
    pallas_call x1, Pallas kernels: 122 us -> 101 us  [local(): pl.pallas_call(functools.partial(kernel, size), out_shape=(jax.ShapeDtype...]
    unnamed x30 -> x2, local copies, waits for them, and re-layouts: 12.5 us -> 2.09 us
where the time goes in v2:
time: 103 us
  Pallas kernels  101 us (98%)
  local copies, waits for them, and re-layouts  2.09 us (2%)
    pallas_call x1, Pallas kernels, local(): pl.pallas_call(functools.partial(kernel, size), out_shape=(jax.ShapeDtype...  101 us
    unnamed x2, local copies, waits for them, and re-layouts  2.09 us

profile of v2, /device:TPU:129, one launch (start us, length us, event | category | flops | bytes accessed | tf_op | source)
XLA Modules:
  0.0 103.3 jit_solution(5282411670712655034)
XLA Ops:
  0.6 100.5 %shard_map.158 = (bf16[16,160]{1,0:T(8,128)(2,1)S(1)}, f32[16,320,128]{2,1,0:T(8,128)S(1)}) custom-call(s32[16]{0:T(128)} %len_h.1, s32[16]{0:T(128)} %slot_h.1, f32[1,5]{1,0:T(1,128)} %rate_h.1, f32[1,5]{1,0:T(1,128)} %bias_h.1, f32[1,5]{1,0:T(1,128)} %skip_h.1, bf16[16,160]{1,0:T(8,128)(2,1)} %hid_h.1, f32[1,2560]{1,0:T(1,128)} %gain_h.1, ...), custom_call_target="tpu_custom_call" | custom-call | tf_op jit(solution)/shard_map/pallas_call | solution.py:660
  101.2 0.6 copy.19
  101.8 1.5 %copy.20 = f32[1,16,5,64,128]{4,3,2,1,0:T(8,128)} copy(f32[1,16,5,64,128]{4,3,2,1,0:T(8,128)S(1)} %bitcast.13) | data formatting | bytes 5242880

commit v3 on v2

--- a/solution.py
+++ b/solution.py
@@ -104,6 +104,7 @@
     send_sem,
     x_sem,
     w_sem,
+    g_sem,
     s_sem,
     m_sem,
     b_sem,
@@ -114,6 +115,11 @@
     nd, nm, ns, rows, feat, chan, head, small, bcw, slots_dev, width, inner = size
     ratio = nm // nd
     pairs = ratio // 2
+    pair = 2 * chan
+    two = 2 * LANES
+    gap = chan - two
+    window = 3 * LANES
+    half = feat // 2
     d = lax.axis_index("dp")
     m = lax.axis_index("mp")
     sec = lax.axis_index("section")
@@ -125,13 +131,17 @@
     all_rows = nd * rows
     heads_dev = chan // head
     first = sec == 0
-    last = sec == ns - 1
+    later = sec > 0
+    more = sec < ns - 1
+    after = jnp.minimum(sec + 1, ns - 1)
+    my_rows = pl.ds(pl.multiple_of(d * rows, rows), rows)
+    far_first = (2, 1, 3, 0) if nd == 4 else tuple(range(nd))
 
     srcs = (
         (hid_h, hid),
         (gain_h, gain),
         (wb_h, wb),
-        (w_h, w),
+        (w_h, w.at[d]),
         (cxw_h, cxw),
         (cbw_h, cbw),
         (cxp_h, cxp),
@@ -160,84 +170,209 @@
             barrier, inc=1, device_id=where, device_id_type=pl.DeviceIdType.MESH
         )
 
-    for i in range(nm):
-
-        @pl.when(jnp.logical_not(on_home & (m == i)))
-        def _():
-            tell(home, i)
-
-    for i in range(nd):
-        for j in range(ratio):
-
-            @pl.when(jnp.logical_not((d == i) & (m == d * ratio + j)))
-            def _():
-                tell(i, d * ratio + j)
-
     for k in range(1, nd):
         tell(lax.rem(d + k, nd), m)
     for k in range(1, nm):
         tell(d, lax.rem(m + k, nm))
 
-    @pl.when(sec > 0)
+    @pl.when(first)
+    def _():
+        for i in range(nm):
+
+            @pl.when(jnp.logical_not(on_home & (m == i)))
+            def _():
+                tell(home, i)
+
+        for i in range(nd):
+            for j in range(ratio):
+
+                @pl.when(jnp.logical_not((d == i) & (m == d * ratio + j)))
+                def _():
+                    tell(i, d * ratio + j)
+
+    @pl.when(sec == 1)
     def _():
         for k in range(nd):
-            tell(k, m, sec - 1)
+            tell(k, m, 0)
+
+    @pl.when(sec > 1)
+    def _():
+        tell(d, m, sec - 1)
 
     own = jnp.where(on_home, 1, 0)
     pl.semaphore_wait(
-        barrier, 2 * (nm - own) + nd - 1 + nm - 1 + jnp.where(sec < ns - 1, nd, 0)
-    )
-
-    sent = []
-
-    def send(src, dst, recv, where, self_too=None, only=None):
-        sem = send_sem.at[len(sent)]
-        copy = pltpu.make_async_remote_copy(
+        barrier,
+        nd
+        - 1
+        + nm
+        - 1
+        + jnp.where(first, 2 * (nm - own) + nd, jnp.where(more, 1, 0)),
+    )
+
+    count = 0
+    bases = {}
+    for name, n in (
+        ("x", nd - 1),
+        ("w", nd - 1),
+        ("g", 8),
+        ("s", nm - 1),
+        ("m", nm),
+        ("b", nm),
+        ("c", nd),
+        ("h", 1),
+        ("o", nd - 1),
+    ):
+        bases[name] = count
+        count += n
+
+    def block_of(i):
+        return pl.ds(pl.multiple_of(i * rows, rows), rows)
+
+    def copies_x():
+        for k in range(1, nd):
+            there = {"dp": lax.rem(d + k, nd), "mp": m}
+            yield hid, recv_x.at[my_rows], x_sem.at[d], there, None
+
+    def copies_w():
+        for k in range(1, nd):
+            there = {"dp": lax.rem(d + k, nd), "mp": m}
+            yield wg.at[d], wg.at[d], w_sem.at[d], there, None
+
+    up = lax.rem(d + 1, nd)
+    down = lax.rem(d + nd - 1, nd)
+    across = lax.rem(d + 2, nd)
+
+    parts = (slice(0, 2), slice(2, 3))
+
+    def copies_g(part):
+        at = parts[part]
+        yield w.at[d, at], w.at[d, at], g_sem.at[part, 0], {"dp": up, "mp": m}, None
+        if nd == 4:
+            yield w.at[d, at], w.at[d, at], g_sem.at[part, 1], {"dp": down, "mp": m}, None
+
+    def copies_g2(part, which):
+        at = parts[part]
+        if which == 0:
+            block = w.at[down, at, 0:half]
+            yield block, block, g_sem.at[part, 2], {"dp": up, "mp": m}, None
+        else:
+            block = w.at[up, at, half:feat]
+            yield block, block, g_sem.at[part, 3], {"dp": down, "mp": m}, None
+
+    def pass_on(part):
+        at = parts[part]
+        arrived(w.at[down, at], g_sem.at[part, 0])
+        if nd == 4:
+            start(bases["g"] + 4 * part + 2, copies_g2(part, 0))
+            arrived(w.at[up, at], g_sem.at[part, 1])
+            start(bases["g"] + 4 * part + 3, copies_g2(part, 1))
+
+    def passed_on(part):
+        at = parts[part]
+        if nd == 4:
+            arrived(w.at[across, at, 0:half], g_sem.at[part, 2])
+            arrived(w.at[across, at, half:feat], g_sem.at[part, 3])
+
+    def copies_s():
+        for k in range(1, nm):
+            there = {"dp": d, "mp": lax.rem(m + k, nm)}
+            yield send_s, recv_s.at[m], s_sem.at[m], there, None
+
+    def copies_m_first(p):
+        for k in far_first:
+            i = lax.rem(d + k, nd)
+            for j in (2 * p, 2 * p + 1):
+                there = {"dp": i, "mp": d * ratio + j}
+                same = (i == d) & (m == d * ratio + j)
+                yield send_m.at[j * nd + i], recv_m.at[m], m_sem.at[m], there, same
+
+    def copies_m_later(k, p):
+        i = lax.rem(home + k, nd)
+        for j in (2 * p, 2 * p + 1):
+            to = i * ratio + j
+            yield send_m.at[to], recv_m.at[m], m_sem.at[m], {"dp": d, "mp": to}, to == m
+
+    def copies_b_first():
+        for k in range(nm):
+            i = lax.rem(m + nm // 2 + k, nm)
+            slot = mine * nd + d
+            there = {"dp": home, "mp": i}
+            yield send_b, recv_b.at[slot], b_sem.at[slot], there, on_home & (m == i)
+
+    def copies_b_later():
+        for k in range(nm):
+            i = lax.rem(m + nm // 2 + k, nm)
+            yield send_b, recv_b.at[m], b_sem.at[m], {"dp": d, "mp": i}, i == m
+
+    def copies_c():
+        for k in far_first:
+            i = lax.rem(d + k, nd)
+            there = {"dp": i, "mp": m, "section": after}
+            yield send_c.at[i], recv_c.at[d], c_sem.at[d], there, None
+
+    def copies_h(src):
+        yield src, recv_h, h_sem.at[0], {"dp": d, "mp": m, "section": after}, None
+
+    def copies_o():
+        for k in range(1, nd):
+            i = lax.rem(d + k, nd)
+            yield send_c.at[i], recv_o.at[d], o_sem.at[d], {"dp": i, "mp": m}, None
+
+    def remote(at, src, dst, recv, where):
+        return pltpu.make_async_remote_copy(
             src_ref=src,
             dst_ref=dst,
-            send_sem=sem,
+            send_sem=send_sem.at[at],
             recv_sem=recv,
             device_id=where,
             device_id_type=pl.DeviceIdType.MESH,
         )
-        if only is not None:
-
-            @pl.when(only)
-            def _():
+
+    def start(base, items):
+        for n, (src, dst, recv, where, same) in enumerate(items):
+            copy = remote(base + n, src, dst, recv, where)
+            if same is None:
                 copy.start()
-
-            sent.append((copy, only))
-        elif self_too is None:
-            copy.start()
-            sent.append((copy, None))
-        else:
-
-            @pl.when(jnp.logical_not(self_too))
-            def _():
-                copy.start()
-
-            @pl.when(self_too)
-            def _():
-                pltpu.make_async_copy(src, dst, recv).start()
-
-            sent.append((copy, jnp.logical_not(self_too)))
+            else:
+
+                @pl.when(jnp.logical_not(same))
+                def _():
+                    copy.start()
+
+                @pl.when(same)
+                def _():
+                    pltpu.make_async_copy(src, dst, recv).start()
+
+    def finish(base, items):
+        for n, (src, dst, recv, where, same) in enumerate(items):
+            copy = remote(base + n, src, dst, recv, where)
+            if same is None:
+                copy.wait_send()
+            else:
+
+                @pl.when(jnp.logical_not(same))
+                def _():
+                    copy.wait_send()
 
     def arrived(ref, sem):
         pltpu.make_async_copy(ref, ref, sem).wait()
 
     loads[0].wait()
+
+    @pl.when(first)
+    def _():
+        start(bases["x"], copies_x())
+
     loads[2].wait()
     group_w = wg.shape[2]
     wg[d] = jnp.zeros((feat, group_w), BF16)
     wg[d, :, 0:per_dp] = wb[...]
-    my_rows = pl.ds(pl.multiple_of(d * rows, rows), rows)
-    for k in range(1, nd):
-        there = {"dp": lax.rem(d + k, nd), "mp": m}
-        send(wg.at[d], wg.at[d], w_sem.at[d], there)
-    for k in range(1, nd):
-        there = {"dp": lax.rem(d + k, nd), "mp": m}
-        send(hid, recv_x.at[my_rows], x_sem.at[d], there)
-    recv_x[my_rows, :] = hid[...]
+    start(bases["w"], copies_w())
+    loads[3].wait()
+
+    @pl.when(later)
+    def _():
+        start(bases["g"], copies_g(0))
 
     col = iota(perm.shape, 1)
     row = iota(perm.shape, 0)
@@ -256,11 +391,9 @@
     loads[1].wait()
     offset = m * feat
     base = offset // LANES
-    gain_w = gain[:, pl.ds(pl.multiple_of(base * LANES, LANES), 2 * LANES)]
-    gain_w = jnp.broadcast_to(gain_w, (8, 2 * LANES))
-    gain_w = pltpu.roll(
-        gain_w, lax.rem(2 * LANES - (offset - base * LANES), 2 * LANES), 1
-    )
+    gain_w = gain[:, pl.ds(pl.multiple_of(base * LANES, LANES), two)]
+    gain_w = jnp.broadcast_to(gain_w, (8, two))
+    gain_w = pltpu.roll(gain_w, lax.rem(two - (offset - base * LANES), two), 1)
     gain_row = gain_w[0:1, 0:feat]
 
     for k in range(1, nd):
@@ -270,10 +403,6 @@
     for i in range(1, nd):
         total += mm(wg[i], perm[i * group_w : (i + 1) * group_w, :])
     wsmall[...] = total.astype(BF16)
-    for k in range(1, nd):
-        i = lax.rem(d + k, nd)
-        block = pl.ds(pl.multiple_of(i * rows, rows), rows)
-        arrived(recv_x.at[block], x_sem.at[i])
 
     def prepare():
         for copy in loads[4:9] + loads[10:]:
@@ -299,78 +428,93 @@
 
         lax.fori_loop(0, rows, one, 0)
 
-    @pl.when(first)
-    def _():
-        h[...] = recv_x[...]
-
-    @pl.when(jnp.logical_not(first))
-    def _():
-        prepare()
-        arrived(recv_h, h_sem.at[0])
-        acc = None
-        for i in range(nd):
-            arrived(recv_c.at[i], c_sem.at[i])
-            part = recv_c[i].astype(F32)
-            acc = part if acc is None else acc + part
+    def after_norm(acc, residual):
         lane = iota(acc.shape, 1)
         squares = jnp.sum(
             jnp.where((lane == feat) | (lane == feat + 1), acc, 0.0), axis=1, keepdims=True
         )
         scale = lax.rsqrt(squares / inner + EPS)
-        h[...] = (recv_h[...].astype(F32) + acc[:, 0:feat] * scale).astype(BF16)
-
-    value = h[my_rows, :].astype(F32)
+        return (residual.astype(F32) + acc[:, 0:feat] * scale).astype(BF16)
+
+    @pl.when(first)
+    def _():
+        h[...] = hid[...]
+
+    @pl.when(later)
+    def _():
+        prepare()
+        pass_on(0)
+        start(bases["g"] + 4, copies_g(1))
+        passed_on(0)
+        arrived(recv_h, h_sem.at[0])
+
+        @pl.when(sec == 1)
+        def _():
+            acc = None
+            for i in range(nd):
+                arrived(recv_c.at[i], c_sem.at[i])
+                part = recv_c[i].astype(F32)
+                acc = part if acc is None else acc + part
+            h[...] = after_norm(acc, recv_h[...])
+
+        @pl.when(sec > 1)
+        def _():
+            h[...] = recv_h[...]
+
+    value = h[...].astype(F32)
     squares = jnp.sum(value * value, axis=1, keepdims=True)
-    out = mm((value * gain_row).astype(BF16), wsmall[...])
+    v = (value * gain_row).astype(BF16)
+    out = mm(v, wsmall[...])
     high, low = halves(squares)
     lane = iota(out.shape, 1)
     out = jnp.where(lane == small, high, jnp.where(lane == small + 1, low, out))
     send_s[...] = out.astype(BF16)
-    for k in range(1, nm):
-        there = {"dp": d, "mp": lax.rem(m + k, nm)}
-        send(send_s, recv_s.at[m], s_sem.at[m], there)
+    start(bases["s"], copies_s())
     recv_s[m] = send_s[...]
-    v = (h[...].astype(F32) * gain_row).astype(BF16)
-    loads[3].wait()
-    pair = 2 * chan
-    two = 2 * LANES
-    gap = chan - two
-    window = 3 * LANES
-    lane = iota((all_rows, LANES), 1)
-    for p in range(pairs):
-        at = p * pair
-        cols = slice(at, at + pair)
-        inner_p = mm(v, w[1, :, cols])
-        gate_p = mm(v, w[0, :, cols])
+
+    def pack(inner_p, gate_p, even, other, shape):
+        lane = iota((inner_p.shape[0], LANES), 1)
         inner_t = inner_p[:, two:window]
         gate_t = pltpu.roll(gate_p[:, two:window], gap, 1)
-        send_m[2 * p, :, 0:two] = inner_p[:, 0:two].astype(BF16)
-        send_m[2 * p, :, two : 2 * two] = gate_p[:, 0:two].astype(BF16)
-        send_m[2 * p, :, 2 * two :] = jnp.where(lane < gap, inner_t, gate_t).astype(BF16)
-        send_m[2 * p + 1, :, 0:two] = inner_p[:, window:].astype(BF16)
-        send_m[2 * p + 1, :, two : 2 * two] = gate_p[:, window:].astype(BF16)
-        send_m[2 * p + 1, :, 2 * two :] = jnp.where(lane < gap, gate_t, inner_t).astype(BF16)
-        for k in (2, 1, 3, 0) if nd == 4 else range(nd):
+        for at, side, edge in (
+            (even, slice(0, two), jnp.where(lane < gap, inner_t, gate_t)),
+            (other, slice(window, pair), jnp.where(lane < gap, gate_t, inner_t)),
+        ):
+            send_m[at, :, 0:two] = inner_p[:, side].astype(BF16).reshape(*shape, two)
+            send_m[at, :, two : 2 * two] = gate_p[:, side].astype(BF16).reshape(*shape, two)
+            send_m[at, :, 2 * two :] = edge.astype(BF16).reshape(*shape, LANES)
+
+    @pl.when(first)
+    def _():
+        for k in range(1, nd):
             i = lax.rem(d + k, nd)
-            block = pl.ds(pl.multiple_of(i * rows, rows), rows)
-            for e in range(2):
-                j = 2 * p + e
-                there = {"dp": i, "mp": d * ratio + j}
-                send(
-                    send_m.at[j, block],
-                    recv_m.at[m],
-                    m_sem.at[m],
-                    there,
-                    (i == d) & (m == d * ratio + j),
-                )
-
-    more = jnp.logical_not(last)
-    after = jnp.minimum(sec + 1, ns - 1)
-    send(h, recv_h, h_sem.at[0], {"dp": d, "mp": m, "section": after}, only=more)
-
-    @pl.when(first)
-    def _():
+            arrived(recv_x.at[block_of(i)], x_sem.at[i])
+        recv_x[my_rows, :] = hid[...]
+        v_all = (recv_x[...].astype(F32) * gain_row).astype(BF16)
+        for p in range(pairs):
+            cols = slice(p * pair, (p + 1) * pair)
+            e = 2 * p * nd
+            pack(
+                mm(v_all, w[d, 1, :, cols]),
+                mm(v_all, w[d, 0, :, cols]),
+                slice(e, e + nd),
+                slice(e + nd, e + 2 * nd),
+                (nd, rows),
+            )
+            start(bases["m"] + e, copies_m_first(p))
+        start(bases["h"], copies_h(h))
         prepare()
+
+    @pl.when(later)
+    def _():
+        for n, k in enumerate(far_first):
+            i = lax.rem(home + k, nd)
+            for p in range(pairs):
+                cols = slice(p * pair, (p + 1) * pair)
+                e = i * ratio + 2 * p
+                pack(mm(v, w[i, 1, :, cols]), mm(v, w[i, 0, :, cols]), e, e + 1, (rows,))
+                start(bases["m"] + n * ratio + 2 * p, copies_m_later(k, p))
+        pass_on(1)
 
     loads[9].wait()
     per_head = iota((1, chan), 1) // head
@@ -422,8 +566,8 @@
 
     def in_order(part, edge):
         before = jnp.concatenate([edge, part], axis=1)
-        after = jnp.concatenate([part, edge], axis=1)
-        return jnp.where(odd, pltpu.roll(before, chan, 1), after)[:, 0:chan]
+        behind = jnp.concatenate([part, edge], axis=1)
+        return jnp.where(odd, pltpu.roll(before, chan, 1), behind)[:, 0:chan]
 
     acc_i = in_order(acc[:, 0:two], tile)
     acc_g = in_order(acc[:, two : 2 * two], other)
@@ -438,16 +582,14 @@
     full = jnp.where(lane == chan, high, jnp.where(lane == chan + 1, low, full))
     full = jnp.where(odd, pltpu.roll(full, window - chan, 1), full)
     send_b[...] = full.astype(BF16)
-    for k in range(nm):
-        i = lax.rem(m + k, nm)
-        there = {"dp": home, "mp": i}
-        send(
-            send_b,
-            recv_b.at[mine, my_rows],
-            b_sem.at[mine * nd + d],
-            there,
-            on_home & (m == i),
-        )
+
+    @pl.when(first)
+    def _():
+        start(bases["b"], copies_b_first())
+
+    @pl.when(later)
+    def _():
+        start(bases["b"], copies_b_later())
 
     s_high, s_low = halves(sx)
     d_high, d_low = halves(decay)
@@ -468,7 +610,7 @@
         axis=1,
     )
     right = jnp.concatenate(
-        [right, jnp.zeros((LANES - 5 * rows, 2 * LANES), F32)], axis=0
+        [right, jnp.zeros((LANES - 5 * rows, two), F32)], axis=0
     ).astype(BF16)
     r_row = lax.rem(iota((LANES, 1), 0), rows)
 
@@ -481,70 +623,108 @@
 
     lax.fori_loop(0, rows // 2, update, 0)
 
-    out = jnp.zeros((all_rows, feat), F32)
-    squares = jnp.zeros((all_rows, 1), F32)
-    lane = iota((all_rows, LANES), 1)
-    for p in range(pairs):
-        for e in range(2):
-            for i in range(nd):
-                arrived(
-                    recv_b.at[2 * p + e, i * rows : (i + 1) * rows],
-                    b_sem.at[(2 * p + e) * nd + i],
-                )
-        even_t = recv_b[2 * p, :, 2 * LANES : 3 * LANES].astype(F32)
-        odd_t = recv_b[2 * p + 1, :, 0:LANES].astype(F32)
-        squares += jnp.sum(
+    def gathered(even_s, other_s, count):
+        n = count * rows
+        lane = iota((n, LANES), 1)
+        even_t = recv_b[even_s, :, two:window].astype(F32).reshape(n, LANES)
+        odd_t = recv_b[other_s, :, 0:LANES].astype(F32).reshape(n, LANES)
+        squares = jnp.sum(
             jnp.where((lane == gap) | (lane == gap + 1), even_t, 0.0)
             + jnp.where(lane < 2, odd_t, 0.0),
             axis=1,
             keepdims=True,
         )
         middle = jnp.where(lane < gap, even_t, odd_t).astype(BF16)
-        at = p * pair
-        out += mm_t(recv_b[2 * p, :, 0 : 2 * LANES], w[2, :, at : at + 2 * LANES])
-        out += mm_t(middle, w[2, :, at + 2 * LANES : at + 3 * LANES])
-        out += mm_t(recv_b[2 * p + 1, :, LANES:window], w[2, :, at + 3 * LANES : at + pair])
-    wide_c[:, 0:feat] = out
-    full = wide_c[...]
-    high, low = halves(squares)
-    lane = iota(full.shape, 1)
-    full = jnp.where(lane == feat, high, jnp.where(lane == feat + 1, low, full))
-    send_c[...] = full.astype(BF16)
-
-    for k in range(nd):
-        there = {"dp": lax.rem(d + k, nd), "mp": m, "section": after}
-        send(send_c, recv_c.at[d], c_sem.at[d], there, only=more)
-    for k in range(1, nd):
-        i = lax.rem(d + k, nd)
-        block = pl.ds(pl.multiple_of(i * rows, rows), rows)
-        send(send_c.at[block], recv_o.at[d], o_sem.at[d], {"dp": i, "mp": m})
-    recv_o[d] = send_c[my_rows, :]
+        left = recv_b[even_s, :, 0:two].reshape(n, two)
+        right = recv_b[other_s, :, LANES:window].reshape(n, two)
+        return jnp.concatenate([left, middle, right], axis=1), squares
+
+    def with_squares(out, squares, n):
+        wide_c[0:n, 0:feat] = out
+        full = wide_c[0:n, :]
+        high, low = halves(squares)
+        lane = iota(full.shape, 1)
+        return jnp.where(lane == feat, high, jnp.where(lane == feat + 1, low, full))
+
+    @pl.when(first)
+    def _():
+        out = jnp.zeros((all_rows, feat), F32)
+        squares = jnp.zeros((all_rows, 1), F32)
+        for p in range(pairs):
+            e = 2 * p * nd
+            for i in range(2 * nd):
+                arrived(recv_b.at[e + i], b_sem.at[e + i])
+            lhs, part = gathered(slice(e, e + nd), slice(e + nd, e + 2 * nd), nd)
+            squares += part
+            out += mm_t(lhs, w[d, 2, :, p * pair : (p + 1) * pair])
+        full = with_squares(out, squares, all_rows)
+        send_c[...] = full.astype(BF16).reshape(nd, rows, two)
+        start(bases["c"], copies_c())
+        start(bases["o"], copies_o())
+        recv_o[d] = send_c[d]
+
+    @pl.when(later)
+    def _():
+        passed_on(1)
+        out = jnp.zeros((rows, feat), F32)
+        squares = jnp.zeros((rows, 1), F32)
+        for i in range(nd):
+            for p in range(pairs):
+                e = i * ratio + 2 * p
+                arrived(recv_b.at[e], b_sem.at[e])
+                arrived(recv_b.at[e + 1], b_sem.at[e + 1])
+                lhs, part = gathered(e, e + 1, 1)
+                squares += part
+                out += mm_t(lhs, w[i, 2, :, p * pair : (p + 1) * pair])
+        hid_new[...] = after_norm(with_squares(out, squares, rows), h[...])
+
+        @pl.when(more)
+        def _():
+            start(bases["h"], copies_h(hid_new))
 
     lax.fori_loop(rows // 2, rows, update, 0)
 
-    for k in range(1, nd):
-        i = lax.rem(d + k, nd)
-        arrived(recv_o.at[i], o_sem.at[i])
-    acc = recv_o[0].astype(F32)
-    for i in range(1, nd):
-        acc += recv_o[i].astype(F32)
-    lane = iota(acc.shape, 1)
-    squares = jnp.sum(
-        jnp.where((lane == feat) | (lane == feat + 1), acc, 0.0), axis=1, keepdims=True
-    )
-    scale = lax.rsqrt(squares / inner + EPS)
-    hid_new[...] = (h[my_rows, :].astype(F32) + acc[:, 0:feat] * scale).astype(BF16)
+    @pl.when(first)
+    def _():
+        for k in range(1, nd):
+            i = lax.rem(d + k, nd)
+            arrived(recv_o.at[i], o_sem.at[i])
+        acc = recv_o[0].astype(F32)
+        for i in range(1, nd):
+            acc += recv_o[i].astype(F32)
+        hid_new[...] = after_norm(acc, h[...])
+
     result = pltpu.make_async_copy(hid_new, hid_o, out_sem.at[0])
     result.start()
 
-    for copy, cond in sent:
-        if cond is None:
-            copy.wait_send()
-        else:
-
-            @pl.when(cond)
-            def _():
-                copy.wait_send()
+    finish(bases["w"], copies_w())
+    finish(bases["s"], copies_s())
+
+    @pl.when(first)
+    def _():
+        finish(bases["x"], copies_x())
+        for p in range(pairs):
+            finish(bases["m"] + 2 * p * nd, copies_m_first(p))
+        finish(bases["h"], copies_h(h))
+        finish(bases["b"], copies_b_first())
+        finish(bases["c"], copies_c())
+        finish(bases["o"], copies_o())
+
+    @pl.when(later)
+    def _():
+        for part in (0, 1):
+            finish(bases["g"] + 4 * part, copies_g(part))
+            if nd == 4:
+                finish(bases["g"] + 4 * part + 2, copies_g2(part, 0))
+                finish(bases["g"] + 4 * part + 3, copies_g2(part, 1))
+        for n, k in enumerate(far_first):
+            for p in range(pairs):
+                finish(bases["m"] + n * ratio + 2 * p, copies_m_later(k, p))
+        finish(bases["b"], copies_b_later())
+
+        @pl.when(more)
+        def _():
+            finish(bases["h"], copies_h(hid_new))
 
     def drain(s, carry):
         pltpu.make_async_copy(new.at[s], st_o.at[s], store_sem.at[s]).wait()
@@ -605,16 +785,20 @@
         state_pool.reshape(slots_dev, chan, state),
         gate_gain,
     )
-    sends = 2 * (nd - 1) + nd * ratio + 2 * nm - 1 + 2 * nd
+    sends = 4 * nd + 3 * nm + 5
     dma = pltpu.SemaphoreType.DMA
     scratch = (
         [pltpu.SMEM(a.shape, a.dtype) for a in operands[:5]]
-        + [pltpu.VMEM(a.shape, a.dtype) for a in operands[5:]]
+        + [
+            pltpu.VMEM((nd, *a.shape) if i == 7 else a.shape, a.dtype)
+            for i, a in enumerate(operands)
+            if i >= 5
+        ]
         + [
             pltpu.VMEM((nd, feat, group_w), BF16),
             pltpu.VMEM((nd * group_w, small_pad), BF16),
             pltpu.VMEM((feat, small_pad), BF16),
-            pltpu.VMEM((all_rows, feat), BF16),
+            pltpu.VMEM((rows, feat), BF16),
             pltpu.VMEM((rows, chan), F32),
             pltpu.VMEM((rows, bcw), F32),
             pltpu.VMEM((rows, LANES), F32),
@@ -629,17 +813,17 @@
         ]
         + [
             pltpu.VMEM((rows, small_pad), BF16),
-            pltpu.VMEM((ratio, all_rows, 2 * chan), BF16),
+            pltpu.VMEM((nm, rows, 2 * chan), BF16),
             pltpu.VMEM((rows, window), BF16),
-            pltpu.VMEM((all_rows, 2 * LANES), BF16),
+            pltpu.VMEM((nd, rows, 2 * LANES), BF16),
         ]
         + [
             pltpu.VMEM((all_rows, feat), BF16),
             pltpu.VMEM((nm, rows, small_pad), BF16),
             pltpu.VMEM((nm, rows, 2 * chan), BF16),
-            pltpu.VMEM((ratio, all_rows, window), BF16),
-            pltpu.VMEM((nd, all_rows, 2 * LANES), BF16),
-            pltpu.VMEM((all_rows, feat), BF16),
+            pltpu.VMEM((nm, rows, window), BF16),
+            pltpu.VMEM((nd, rows, 2 * LANES), BF16),
+            pltpu.VMEM((rows, feat), BF16),
             pltpu.VMEM((nd, rows, 2 * LANES), BF16),
         ]
         + [
@@ -649,6 +833,7 @@
             dma((sends,)),
             dma((nd,)),
             dma((nd,)),
+            dma((2, 4)),
             dma((nm,)),
             dma((nm,)),
             dma((nd * ratio,)),

time: 103 us -> 89.8 us (0.87)
  Pallas kernels: 101 us -> 87 us
    pallas_call x1, Pallas kernels: 101 us -> 87 us  [local(): pl.pallas_call(functools.partial(kernel, size), out_shape=(jax.ShapeDtype...]
where the time goes in v3:
time: 89.8 us; the launch traced here: 89.7 us
  Pallas kernels  87 us (97%)
  local copies, waits for them, and re-layouts  2.09 us (2%)
    pallas_call x1, Pallas kernels, local(): pl.pallas_call(functools.partial(kernel, size), out_shape=(jax.ShapeDtype...  87 us
    unnamed x2, local copies, waits for them, and re-layouts  2.09 us

profile of v3, /device:TPU:129, one launch (start us, length us, event | category | flops | bytes accessed | tf_op | source)
XLA Modules:
  0.0 89.7 jit_solution(12624650888371459929)
XLA Ops:
  0.6 87.0 %shard_map.158 = (bf16[16,160]{1,0:T(8,128)(2,1)S(1)}, f32[16,320,128]{2,1,0:T(8,128)S(1)}) custom-call(s32[16]{0:T(128)} %len_h.1, s32[16]{0:T(128)} %slot_h.1, f32[1,5]{1,0:T(1,128)} %rate_h.1, f32[1,5]{1,0:T(1,128)} %bias_h.1, f32[1,5]{1,0:T(1,128)} %skip_h.1, bf16[16,160]{1,0:T(8,128)(2,1)} %hid_h.1, f32[1,2560]{1,0:T(1,128)} %gain_h.1, ...), custom_call_target="tpu_custom_call" | custom-call | tf_op jit(solution)/shard_map/pallas_call | solution.py:845
  87.6 0.6 copy.19
  88.2 1.5 %copy.20 = f32[1,16,5,64,128]{4,3,2,1,0:T(8,128)} copy(f32[1,16,5,64,128]{4,3,2,1,0:T(8,128)S(1)} %bitcast.13) | data formatting | bytes 5242880

commit v4 on v3

--- a/solution.py
+++ b/solution.py
@@ -85,7 +85,6 @@
     wide_c,
     outer_l,
     outer_t,
-    new,
     hid_new,
     send_s,
     send_m,
@@ -99,8 +98,6 @@
     recv_h,
     recv_o,
     load_sem,
-    store_sem,
-    out_sem,
     send_sem,
     x_sem,
     w_sem,
@@ -157,8 +154,8 @@
     loads = [
         pltpu.make_async_copy(src, dst, load_sem.at[i]) for i, (src, dst) in enumerate(srcs)
     ]
-    for copy in loads:
-        copy.start()
+    loads[0].start()
+    loads[2].start()
 
     barrier = pltpu.get_barrier_semaphore()
 
@@ -198,6 +195,10 @@
     @pl.when(sec > 1)
     def _():
         tell(d, m, sec - 1)
+
+    loads[3].start()
+    for i in (1, *range(4, len(loads))):
+        loads[i].start()
 
     own = jnp.where(on_home, 1, 0)
     pl.semaphore_wait(
@@ -215,7 +216,7 @@
         ("x", nd - 1),
         ("w", nd - 1),
         ("g", 8),
-        ("s", nm - 1),
+        ("s", nm),
         ("m", nm),
         ("b", nm),
         ("c", nd),
@@ -273,8 +274,10 @@
             arrived(w.at[across, at, 0:half], g_sem.at[part, 2])
             arrived(w.at[across, at, half:feat], g_sem.at[part, 3])
 
+    others = sorted(range(1, nm), key=lambda k: abs(k - nm // 2))
+
     def copies_s():
-        for k in range(1, nm):
+        for k in others:
             there = {"dp": d, "mp": lax.rem(m + k, nm)}
             yield send_s, recv_s.at[m], s_sem.at[m], there, None
 
@@ -283,14 +286,15 @@
             i = lax.rem(d + k, nd)
             for j in (2 * p, 2 * p + 1):
                 there = {"dp": i, "mp": d * ratio + j}
-                same = (i == d) & (m == d * ratio + j)
+                same = m == d * ratio + j if k == 0 else None
                 yield send_m.at[j * nd + i], recv_m.at[m], m_sem.at[m], there, same
 
     def copies_m_later(k, p):
         i = lax.rem(home + k, nd)
         for j in (2 * p, 2 * p + 1):
             to = i * ratio + j
-            yield send_m.at[to], recv_m.at[m], m_sem.at[m], {"dp": d, "mp": to}, to == m
+            same = to == m if k == 0 else None
+            yield send_m.at[to], recv_m.at[m], m_sem.at[m], {"dp": d, "mp": to}, same
 
     def copies_b_first():
         for k in range(nm):
@@ -300,9 +304,9 @@
             yield send_b, recv_b.at[slot], b_sem.at[slot], there, on_home & (m == i)
 
     def copies_b_later():
-        for k in range(nm):
-            i = lax.rem(m + nm // 2 + k, nm)
-            yield send_b, recv_b.at[m], b_sem.at[m], {"dp": d, "mp": i}, i == m
+        for k in others:
+            there = {"dp": d, "mp": lax.rem(m + k, nm)}
+            yield send_b, recv_b.at[m], b_sem.at[m], there, None
 
     def copies_c():
         for k in far_first:
@@ -396,14 +400,6 @@
     gain_w = pltpu.roll(gain_w, lax.rem(two - (offset - base * LANES), two), 1)
     gain_row = gain_w[0:1, 0:feat]
 
-    for k in range(1, nd):
-        i = lax.rem(d + k, nd)
-        arrived(wg.at[i], w_sem.at[i])
-    total = mm(wg[0], perm[0:group_w, :])
-    for i in range(1, nd):
-        total += mm(wg[i], perm[i * group_w : (i + 1) * group_w, :])
-    wsmall[...] = total.astype(BF16)
-
     def prepare():
         for copy in loads[4:9] + loads[10:]:
             copy.wait()
@@ -436,42 +432,6 @@
         scale = lax.rsqrt(squares / inner + EPS)
         return (residual.astype(F32) + acc[:, 0:feat] * scale).astype(BF16)
 
-    @pl.when(first)
-    def _():
-        h[...] = hid[...]
-
-    @pl.when(later)
-    def _():
-        prepare()
-        pass_on(0)
-        start(bases["g"] + 4, copies_g(1))
-        passed_on(0)
-        arrived(recv_h, h_sem.at[0])
-
-        @pl.when(sec == 1)
-        def _():
-            acc = None
-            for i in range(nd):
-                arrived(recv_c.at[i], c_sem.at[i])
-                part = recv_c[i].astype(F32)
-                acc = part if acc is None else acc + part
-            h[...] = after_norm(acc, recv_h[...])
-
-        @pl.when(sec > 1)
-        def _():
-            h[...] = recv_h[...]
-
-    value = h[...].astype(F32)
-    squares = jnp.sum(value * value, axis=1, keepdims=True)
-    v = (value * gain_row).astype(BF16)
-    out = mm(v, wsmall[...])
-    high, low = halves(squares)
-    lane = iota(out.shape, 1)
-    out = jnp.where(lane == small, high, jnp.where(lane == small + 1, low, out))
-    send_s[...] = out.astype(BF16)
-    start(bases["s"], copies_s())
-    recv_s[m] = send_s[...]
-
     def pack(inner_p, gate_p, even, other, shape):
         lane = iota((inner_p.shape[0], LANES), 1)
         inner_t = inner_p[:, two:window]
@@ -484,12 +444,42 @@
             send_m[at, :, two : 2 * two] = gate_p[:, side].astype(BF16).reshape(*shape, two)
             send_m[at, :, 2 * two :] = edge.astype(BF16).reshape(*shape, LANES)
 
+    def with_two(out, squares, at):
+        high, low = halves(squares)
+        lane = iota(out.shape, 1)
+        return jnp.where(lane == at, high, jnp.where(lane == at + 1, low, out))
+
+    def two_of(acc, at):
+        lane = iota(acc.shape, 1)
+        return jnp.sum(
+            jnp.where((lane == at) | (lane == at + 1), acc, 0.0), axis=1, keepdims=True
+        )
+
+    def weights_small():
+        for k in range(1, nd):
+            i = lax.rem(d + k, nd)
+            arrived(wg.at[i], w_sem.at[i])
+        total = mm(wg[0], perm[0:group_w, :])
+        for i in range(1, nd):
+            total += mm(wg[i], perm[i * group_w : (i + 1) * group_w, :])
+        wsmall[...] = total.astype(BF16)
+
+    def start_small():
+        value = h[...].astype(F32)
+        squares = jnp.sum(value * value, axis=1, keepdims=True)
+        v = (value * gain_row).astype(BF16)
+        send_s[...] = with_two(mm(v, wsmall[...]), squares, small).astype(BF16)
+        start(bases["s"], copies_s())
+        pltpu.make_async_copy(send_s, recv_s.at[m], s_sem.at[m]).start()
+        return v
+
     @pl.when(first)
     def _():
         for k in range(1, nd):
             i = lax.rem(d + k, nd)
             arrived(recv_x.at[block_of(i)], x_sem.at[i])
         recv_x[my_rows, :] = hid[...]
+        h[...] = hid[...]
         v_all = (recv_x[...].astype(F32) * gain_row).astype(BF16)
         for p in range(pairs):
             cols = slice(p * pair, (p + 1) * pair)
@@ -502,11 +492,34 @@
                 (nd, rows),
             )
             start(bases["m"] + e, copies_m_first(p))
+        weights_small()
+        start_small()
         start(bases["h"], copies_h(h))
         prepare()
 
     @pl.when(later)
     def _():
+        weights_small()
+        prepare()
+        pass_on(0)
+        start(bases["g"] + 4, copies_g(1))
+        passed_on(0)
+        arrived(recv_h, h_sem.at[0])
+
+        @pl.when(sec == 1)
+        def _():
+            acc = None
+            for i in range(nd):
+                arrived(recv_c.at[i], c_sem.at[i])
+                part = recv_c[i].astype(F32)
+                acc = part if acc is None else acc + part
+            h[...] = after_norm(acc, recv_h[...])
+
+        @pl.when(sec > 1)
+        def _():
+            h[...] = recv_h[...]
+
+        v = start_small()
         for n, k in enumerate(far_first):
             i = lax.rem(home + k, nd)
             for p in range(pairs):
@@ -527,16 +540,11 @@
         skip_row = jnp.where(per_head == i, skip_s[0, i], skip_row)
 
     acc = None
-    for k in range(nm):
-        i = lax.rem(m + k, nm)
-        if k > 0:
-            arrived(recv_s.at[i], s_sem.at[i])
+    for i in range(nm):
+        arrived(recv_s.at[i], s_sem.at[i])
         part = recv_s[i].astype(F32)
         acc = part if acc is None else acc + part
-    lane = iota(acc.shape, 1)
-    squares = jnp.sum(
-        jnp.where((lane == small) | (lane == small + 1), acc, 0.0), axis=1, keepdims=True
-    )
+    squares = two_of(acc, small)
     scale = lax.rsqrt(squares / width + EPS)
     conv_b = silu(past_b[...] + acc[:, 0:bcw] * scale * cbw[3:4, :])
     b_cur = conv_b[:, 0 : bcw // 2]
@@ -590,6 +598,7 @@
     @pl.when(later)
     def _():
         start(bases["b"], copies_b_later())
+        pltpu.make_async_copy(send_b, recv_b.at[m], b_sem.at[m]).start()
 
     s_high, s_low = halves(sx)
     d_high, d_low = halves(decay)
@@ -617,11 +626,11 @@
     def update(s, carry):
         slot = jnp.clip(slot_s[s] - d * slots_dev, 0, slots_dev - 1)
         both = mm(outer_t[...], jnp.where(r_row == s, right, jnp.zeros_like(right)))
-        new[s] = both[:, LANES:] * st[slot] + both[:, 0:LANES]
-        pltpu.make_async_copy(new.at[s], st_o.at[s], store_sem.at[s]).start()
+        st_o[s] = both[:, LANES:] * st[slot] + both[:, 0:LANES]
         return carry
 
-    lax.fori_loop(0, rows // 2, update, 0)
+    before = jnp.where(more, rows // 2, rows)
+    lax.fori_loop(0, before, update, 0)
 
     def gathered(even_s, other_s, count):
         n = count * rows
@@ -682,7 +691,7 @@
         def _():
             start(bases["h"], copies_h(hid_new))
 
-    lax.fori_loop(rows // 2, rows, update, 0)
+    lax.fori_loop(before, rows, update, 0)
 
     @pl.when(first)
     def _():
@@ -694,8 +703,7 @@
             acc += recv_o[i].astype(F32)
         hid_new[...] = after_norm(acc, h[...])
 
-    result = pltpu.make_async_copy(hid_new, hid_o, out_sem.at[0])
-    result.start()
+    hid_o[...] = hid_new[...]
 
     finish(bases["w"], copies_w())
     finish(bases["s"], copies_s())
@@ -726,12 +734,19 @@
         def _():
             finish(bases["h"], copies_h(hid_new))
 
-    def drain(s, carry):
-        pltpu.make_async_copy(new.at[s], st_o.at[s], store_sem.at[s]).wait()
-        return carry
-
-    lax.fori_loop(0, rows, drain, 0)
-    result.wait()
+
+def store(parts, hid_v, st_v, hid_o, st_o, sem):
+    n = st_v.shape[0] // parts
+    copies = [pltpu.make_async_copy(hid_v, hid_o, sem.at[parts])] + [
+        pltpu.make_async_copy(
+            st_v.at[i * n : (i + 1) * n], st_o.at[i * n : (i + 1) * n], sem.at[i]
+        )
+        for i in range(parts)
+    ]
+    for copy in copies:
+        copy.start()
+    for copy in copies:
+        copy.wait()
 
 
 def local(
@@ -785,7 +800,7 @@
         state_pool.reshape(slots_dev, chan, state),
         gate_gain,
     )
-    sends = 4 * nd + 3 * nm + 5
+    sends = 4 * nd + 3 * nm + 6
     dma = pltpu.SemaphoreType.DMA
     scratch = (
         [pltpu.SMEM(a.shape, a.dtype) for a in operands[:5]]
@@ -808,7 +823,6 @@
             pltpu.VMEM((all_rows, 2 * LANES), F32),
             pltpu.VMEM((LANES, window), F32),
             pltpu.VMEM((chan, LANES), BF16),
-            pltpu.VMEM((rows, chan, state), F32),
             pltpu.VMEM((rows, feat), BF16),
         ]
         + [
@@ -828,8 +842,6 @@
         ]
         + [
             dma((15,)),
-            dma((rows,)),
-            dma((1,)),
             dma((sends,)),
             dma((nd,)),
             dma((nd,)),
@@ -842,7 +854,7 @@
             dma((nd,)),
         ]
     )
-    hidden, states = pl.pallas_call(
+    inside = pl.pallas_call(
         functools.partial(kernel, size),
         out_shape=(
             jax.ShapeDtypeStruct((rows, feat), BF16),
@@ -851,14 +863,25 @@
         in_specs=[pl.BlockSpec(memory_space=pltpu.HBM)] * 5
         + [pl.BlockSpec(memory_space=pltpu.HBM)] * 10,
         out_specs=(
-            pl.BlockSpec(memory_space=pl.ANY),
-            pl.BlockSpec(memory_space=pl.ANY),
+            pl.BlockSpec(memory_space=pltpu.VMEM),
+            pl.BlockSpec(memory_space=pltpu.VMEM),
         ),
         scratch_shapes=scratch,
         compiler_params=pltpu.CompilerParams(
             collective_id=0, has_side_effects=True, vmem_limit_bytes=48 << 20
         ),
     )(*[pltpu.with_memory_space_constraint(a, pltpu.HBM) for a in operands])
+    hidden, states = pl.pallas_call(
+        functools.partial(store, rows // 2),
+        out_shape=(
+            jax.ShapeDtypeStruct((rows, feat), BF16),
+            jax.ShapeDtypeStruct((rows, chan, state), F32),
+        ),
+        in_specs=[pl.BlockSpec(memory_space=pltpu.VMEM)] * 2,
+        out_specs=(pl.BlockSpec(memory_space=pltpu.HBM),) * 2,
+        scratch_shapes=[dma((1 + rows // 2,))],
+        compiler_params=pltpu.CompilerParams(vmem_limit_bytes=8 << 20),
+    )(*inside)
     return (
         hidden[None],
         states.reshape(1, rows, heads_dev, head, state),

time: 89.8 us -> 83.1 us (0.925)
  Pallas kernels: 87 us -> 82.4 us
  local copies, waits for them, and re-layouts: 2.09 us -> 0 us
    pallas_call x1, Pallas kernels: 87 us -> 80.8 us  [local(): pl.pallas_call(functools.partial(kernel, size), out_shape=(jax.ShapeDtype...]
    unnamed x2 -> x0, local copies, waits for them, and re-layouts: 2.09 us -> none
    pallas_call x0 -> x1, Pallas kernels: none -> 1.56 us  [local(): pl.pallas_call(functools.partial(store, rows // 2), out_shape=(jax.ShapeD...]
where the time goes in v4:
time: 83.1 us; the launch traced here: 83 us
  Pallas kernels  82.4 us (99%)
    pallas_call x1, Pallas kernels, local(): pl.pallas_call(functools.partial(kernel, size), out_shape=(jax.ShapeDtype...  80.8 us

profile of v4, /device:TPU:129, one launch (start us, length us, event | category | flops | bytes accessed | tf_op | source)
XLA Modules:
  0.0 83.0 jit_solution(16366212807401567115)
XLA Ops:
  0.6 80.8 %shard_map.158 = (bf16[16,160]{1,0:T(8,128)(2,1)S(1)}, f32[16,320,128]{2,1,0:T(8,128)S(1)}) custom-call(s32[16]{0:T(128)} %len_h.1, s32[16]{0:T(128)} %slot_h.1, f32[1,5]{1,0:T(1,128)} %rate_h.1, f32[1,5]{1,0:T(1,128)} %bias_h.1, f32[1,5]{1,0:T(1,128)} %skip_h.1, bf16[16,160]{1,0:T(8,128)(2,1)} %hid_h.1, f32[1,2560]{1,0:T(1,128)} %gain_h.1, ...), custom_call_target="tpu_custom_call" | custom-call | tf_op jit(solution)/shard_map/pallas_call | solution.py:857
  81.5 1.6 %shard_map.159 = (bf16[16,160]{1,0:T(8,128)(2,1)}, f32[16,320,128]{2,1,0:T(8,128)}) custom-call(bf16[16,160]{1,0:T(8,128)(2,1)S(1)} %get-tuple-element.6.hid_v, f32[16,320,128]{2,1,0:T(8,128)S(1)} %get-tuple-element.7.st_v), custom_call_target="tpu_custom_call" | custom-call | tf_op jit(solution)/shard_map/pallas_call | solution.py:874

commit v5 on v4

--- a/solution.py
+++ b/solution.py
@@ -86,12 +86,18 @@
     outer_l,
     outer_t,
     hid_new,
+    acc_s,
+    acc_b,
+    acc_m,
     send_s,
+    send_u,
     send_m,
     send_b,
     send_c,
     recv_x,
     recv_s,
+    recv_t,
+    recv_u,
     recv_m,
     recv_b,
     recv_c,
@@ -103,6 +109,8 @@
     w_sem,
     g_sem,
     s_sem,
+    t_sem,
+    u_sem,
     m_sem,
     b_sem,
     c_sem,
@@ -117,6 +125,9 @@
     gap = chan - two
     window = 3 * LANES
     half = feat // 2
+    side = bcw // 2
+    front = wsmall.shape[1] - side
+    mark = small - side
     d = lax.axis_index("dp")
     m = lax.axis_index("mp")
     sec = lax.axis_index("section")
@@ -222,6 +233,8 @@
         ("c", nd),
         ("h", 1),
         ("o", nd - 1),
+        ("t", nd - 1),
+        ("u", ratio - 1),
     ):
         bases[name] = count
         count += n
@@ -276,10 +289,21 @@
 
     others = sorted(range(1, nm), key=lambda k: abs(k - nm // 2))
 
-    def copies_s():
+    def copies_s(lanes):
         for k in others:
             there = {"dp": d, "mp": lax.rem(m + k, nm)}
-            yield send_s, recv_s.at[m], s_sem.at[m], there, None
+            yield send_s.at[:, 0:lanes], recv_s.at[m, :, 0:lanes], s_sem.at[m], there, None
+
+    def copies_t():
+        for k in range(1, nd):
+            to = lax.rem(home + k, nd) * ratio + mine
+            part = send_s.at[:, front:]
+            yield part, recv_t.at[home], t_sem.at[home], {"dp": d, "mp": to}, None
+
+    def copies_u():
+        for k in range(1, ratio):
+            to = home * ratio + lax.rem(mine + k, ratio)
+            yield send_u, recv_u.at[mine], u_sem.at[mine], {"dp": d, "mp": to}, None
 
     def copies_m_first(p):
         for k in far_first:
@@ -287,7 +311,8 @@
             for j in (2 * p, 2 * p + 1):
                 there = {"dp": i, "mp": d * ratio + j}
                 same = m == d * ratio + j if k == 0 else None
-                yield send_m.at[j * nd + i], recv_m.at[m], m_sem.at[m], there, same
+                block = send_m.at[j * nd + i]
+                yield block, recv_m.at[m], m_sem.at[m], there, same
 
     def copies_m_later(k, p):
         i = lax.rem(home + k, nd)
@@ -301,7 +326,8 @@
             i = lax.rem(m + nm // 2 + k, nm)
             slot = mine * nd + d
             there = {"dp": home, "mp": i}
-            yield send_b, recv_b.at[slot], b_sem.at[slot], there, on_home & (m == i)
+            same = on_home if k == nm // 2 else None
+            yield send_b, recv_b.at[slot], b_sem.at[slot], there, same
 
     def copies_b_later():
         for k in others:
@@ -382,9 +408,9 @@
     row = iota(perm.shape, 0)
     group = row // group_w
     inside = row - group * group_w
-    perm[...] = jnp.where(
-        (inside < per_dp) & (col == group * per_dp + inside), 1.0, 0.0
-    ).astype(BF16)
+    source = group * per_dp + inside
+    target = jnp.where(source < side, source + front, source - side)
+    perm[...] = jnp.where((inside < per_dp) & (col == target), 1.0, 0.0).astype(BF16)
     lane_of = iota((LANES, chan), 1) // head
     expand[...] = jnp.where(
         iota((LANES, chan), 0) == m * heads_dev + lane_of, 1.0, 0.0
@@ -442,7 +468,7 @@
         ):
             send_m[at, :, 0:two] = inner_p[:, side].astype(BF16).reshape(*shape, two)
             send_m[at, :, two : 2 * two] = gate_p[:, side].astype(BF16).reshape(*shape, two)
-            send_m[at, :, 2 * two :] = edge.astype(BF16).reshape(*shape, LANES)
+            send_m[at, :, 2 * two : pair] = edge.astype(BF16).reshape(*shape, LANES)
 
     def with_two(out, squares, at):
         high, low = halves(squares)
@@ -464,13 +490,15 @@
             total += mm(wg[i], perm[i * group_w : (i + 1) * group_w, :])
         wsmall[...] = total.astype(BF16)
 
-    def start_small():
+    def start_small(lanes):
         value = h[...].astype(F32)
         squares = jnp.sum(value * value, axis=1, keepdims=True)
         v = (value * gain_row).astype(BF16)
-        send_s[...] = with_two(mm(v, wsmall[...]), squares, small).astype(BF16)
-        start(bases["s"], copies_s())
-        pltpu.make_async_copy(send_s, recv_s.at[m], s_sem.at[m]).start()
+        send_s[...] = with_two(mm(v, wsmall[...]), squares, mark).astype(BF16)
+        start(bases["s"], copies_s(lanes))
+        pltpu.make_async_copy(
+            send_s.at[:, 0:lanes], recv_s.at[m, :, 0:lanes], s_sem.at[m]
+        ).start()
         return v
 
     @pl.when(first)
@@ -493,7 +521,7 @@
             )
             start(bases["m"] + e, copies_m_first(p))
         weights_small()
-        start_small()
+        start_small(front + side)
         start(bases["h"], copies_h(h))
         prepare()
 
@@ -519,7 +547,8 @@
         def _():
             h[...] = recv_h[...]
 
-        v = start_small()
+        v = start_small(front)
+        start(bases["t"], copies_t())
         for n, k in enumerate(far_first):
             i = lax.rem(home + k, nd)
             for p in range(pairs):
@@ -527,6 +556,13 @@
                 e = i * ratio + 2 * p
                 pack(mm(v, w[i, 1, :, cols]), mm(v, w[i, 0, :, cols]), e, e + 1, (rows,))
                 start(bases["m"] + n * ratio + 2 * p, copies_m_later(k, p))
+        acc = send_s[:, front:].astype(F32)
+        for k in range(1, nd):
+            i = lax.rem(home + k, nd)
+            arrived(recv_t.at[i], t_sem.at[i])
+            acc += recv_t[i].astype(F32)
+        send_u[...] = acc.astype(BF16)
+        start(bases["u"], copies_u())
         pass_on(1)
 
     loads[9].wait()
@@ -539,36 +575,60 @@
         bias_row = jnp.where(per_head == i, bias_s[0, i], bias_row)
         skip_row = jnp.where(per_head == i, skip_s[0, i], skip_row)
 
-    acc = None
-    for i in range(nm):
-        arrived(recv_s.at[i], s_sem.at[i])
-        part = recv_s[i].astype(F32)
-        acc = part if acc is None else acc + part
-    squares = two_of(acc, small)
-    scale = lax.rsqrt(squares / width + EPS)
-    conv_b = silu(past_b[...] + acc[:, 0:bcw] * scale * cbw[3:4, :])
-    b_cur = conv_b[:, 0 : bcw // 2]
-    c_cur = conv_b[:, bcw // 2 :]
-    high, low = halves(acc[:, bcw:])
+    def sum_of(ref, sem, lanes):
+        acc = None
+        for i in range(nm):
+            arrived(ref.at[i, :, 0:lanes], sem.at[i])
+            part = ref[i, :, 0:lanes].astype(F32)
+            acc = part if acc is None else acc + part
+        return acc
+
+    @pl.when(first)
+    def _():
+        acc = sum_of(recv_s, s_sem, front + side)
+        acc_s[...] = acc[:, 0:front]
+        acc_b[...] = acc[:, front:]
+
+    @pl.when(later)
+    def _():
+        acc_s[...] = sum_of(recv_s, s_sem, front)
+
+    acc = acc_s[...]
+    scale = lax.rsqrt(two_of(acc, mark) / width + EPS)
+    c_cur = silu(past_b[:, side:] + acc[:, 0:side] * scale * cbw[3:4, side:])
+    c_high, c_low = halves(c_cur)
+    c_two = jnp.concatenate([c_high, c_low], axis=0).astype(BF16)
+    c_row = lax.rem(iota((2 * rows, 1), 0), rows)
+
+    def ask(s, carry):
+        return carry + mm_t(jnp.where(c_row == s, c_two, jnp.zeros_like(c_two)), old16[s])
+
+    both = lax.fori_loop(
+        0, rows, ask, jnp.zeros((2 * rows, chan), F32), unroll=True
+    )
+    read = both[0:rows] + both[rows:]
+    high, low = halves(acc[:, side:])
     raw = mm(high.astype(BF16), expand[...]) + mm(low.astype(BF16), expand[...])
     step = softplus(raw * scale + bias_row)
     decay = jnp.exp(-step * rate_row) * alive[:, 0:1]
-    c_high, c_low = halves(c_cur)
-    c_two = jnp.concatenate([c_high, c_low], axis=0).astype(BF16)
-    c_row = lax.rem(iota((2 * rows, 1), 0), rows)
-
-    def ask(s, carry):
-        return carry + mm_t(jnp.where(c_row == s, c_two, jnp.zeros_like(c_two)), old16[s])
-
-    both = lax.fori_loop(0, rows, ask, jnp.zeros((2 * rows, chan), F32), unroll=4)
-    read = both[0:rows] + both[rows:]
+
+    @pl.when(first)
+    def _():
+        acc_m[...] = sum_of(recv_m, m_sem, pair)
+
+    @pl.when(later)
+    def _():
+        acc = send_u[...].astype(F32)
+        for k in range(1, ratio):
+            i = lax.rem(mine + k, ratio)
+            arrived(recv_u.at[i], u_sem.at[i])
+            acc += recv_u[i].astype(F32)
+        acc_b[...] = acc
+        acc_m[...] = sum_of(recv_m, m_sem, pair)
+
+    b_cur = silu(past_b[:, 0:side] + acc_b[...] * scale * cbw[3:4, 0:side])
     bc_dot = jnp.sum(b_cur * c_cur, axis=1, keepdims=True)
-
-    acc = None
-    for i in range(nm):
-        arrived(recv_m.at[i], m_sem.at[i])
-        part = recv_m[i].astype(F32)
-        acc = part if acc is None else acc + part
+    acc = acc_m[...]
     tile = acc[:, 2 * two :]
     other = pltpu.roll(tile, gap, 1)
 
@@ -706,11 +766,11 @@
     hid_o[...] = hid_new[...]
 
     finish(bases["w"], copies_w())
-    finish(bases["s"], copies_s())
 
     @pl.when(first)
     def _():
         finish(bases["x"], copies_x())
+        finish(bases["s"], copies_s(front + side))
         for p in range(pairs):
             finish(bases["m"] + 2 * p * nd, copies_m_first(p))
         finish(bases["h"], copies_h(h))
@@ -720,6 +780,9 @@
 
     @pl.when(later)
     def _():
+        finish(bases["s"], copies_s(front))
+        finish(bases["t"], copies_t())
+        finish(bases["u"], copies_u())
         for part in (0, 1):
             finish(bases["g"] + 4 * part, copies_g(part))
             if nd == 4:
@@ -775,7 +838,7 @@
     chan = heads_dev * head
     bcw = conv_bc_weight.shape[2]
     small = per_dp * nd
-    small_pad = -(-(small + 2) // LANES) * LANES
+    small_pad = -(-(small - bcw // 2 + 2) // LANES) * LANES + bcw // 2
     group_w = -(-per_dp // LANES) * LANES
     ratio = nm // nd
     all_rows = nd * rows
@@ -800,7 +863,7 @@
         state_pool.reshape(slots_dev, chan, state),
         gate_gain,
     )
-    sends = 4 * nd + 3 * nm + 6
+    sends = 5 * nd + ratio + 3 * nm + 4
     dma = pltpu.SemaphoreType.DMA
     scratch = (
         [pltpu.SMEM(a.shape, a.dtype) for a in operands[:5]]
@@ -824,9 +887,13 @@
             pltpu.VMEM((LANES, window), F32),
             pltpu.VMEM((chan, LANES), BF16),
             pltpu.VMEM((rows, feat), BF16),
+            pltpu.VMEM((rows, small_pad - bcw // 2), F32),
+            pltpu.VMEM((rows, bcw // 2), F32),
+            pltpu.VMEM((rows, 2 * chan), F32),
         ]
         + [
             pltpu.VMEM((rows, small_pad), BF16),
+            pltpu.VMEM((rows, bcw // 2), BF16),
             pltpu.VMEM((nm, rows, 2 * chan), BF16),
             pltpu.VMEM((rows, window), BF16),
             pltpu.VMEM((nd, rows, 2 * LANES), BF16),
@@ -834,6 +901,8 @@
         + [
             pltpu.VMEM((all_rows, feat), BF16),
             pltpu.VMEM((nm, rows, small_pad), BF16),
+            pltpu.VMEM((nd, rows, bcw // 2), BF16),
+            pltpu.VMEM((ratio, rows, bcw // 2), BF16),
             pltpu.VMEM((nm, rows, 2 * chan), BF16),
             pltpu.VMEM((nm, rows, window), BF16),
             pltpu.VMEM((nd, rows, 2 * LANES), BF16),
@@ -847,6 +916,8 @@
             dma((nd,)),
             dma((2, 4)),
             dma((nm,)),
+            dma((nd,)),
+            dma((ratio,)),
             dma((nm,)),
             dma((nd * ratio,)),
             dma((nd,)),

time: 83.1 us -> 82.3 us (level)
  Pallas kernels: 82.4 us -> 81.5 us
    pallas_call x1, Pallas kernels: 80.8 us -> 80 us  [local(): pl.pallas_call(functools.partial(kernel, size), out_shape=(jax.ShapeDtype...]
where the time goes in v5:
time: 82.3 us; the launch traced here: 82.2 us
  Pallas kernels  81.5 us (99%)
    pallas_call x1, Pallas kernels, local(): pl.pallas_call(functools.partial(kernel, size), out_shape=(jax.ShapeDtype...  80 us

profile of v5, /device:TPU:129, one launch (start us, length us, event | category | flops | bytes accessed | tf_op | source)
XLA Modules:
  0.0 82.2 jit_solution(9618928691427784835)
XLA Ops:
  0.6 80.0 %shard_map.158 = (bf16[16,160]{1,0:T(8,128)(2,1)S(1)}, f32[16,320,128]{2,1,0:T(8,128)S(1)}) custom-call(s32[16]{0:T(128)} %len_h.1, s32[16]{0:T(128)} %slot_h.1, f32[1,5]{1,0:T(1,128)} %rate_h.1, f32[1,5]{1,0:T(1,128)} %bias_h.1, f32[1,5]{1,0:T(1,128)} %skip_h.1, bf16[16,160]{1,0:T(8,128)(2,1)} %hid_h.1, f32[1,2560]{1,0:T(1,128)} %gain_h.1, ...), custom_call_target="tpu_custom_call" | custom-call | tf_op jit(solution)/shard_map/pallas_call | solution.py:928
  80.6 1.6 %shard_map.159 = (bf16[16,160]{1,0:T(8,128)(2,1)}, f32[16,320,128]{2,1,0:T(8,128)}) custom-call(bf16[16,160]{1,0:T(8,128)(2,1)S(1)} %get-tuple-element.6.hid_v, f32[16,320,128]{2,1,0:T(8,128)S(1)} %get-tuple-element.7.st_v), custom_call_target="tpu_custom_call" | custom-call | tf_op jit(solution)/shard_map/pallas_call | solution.py:945

commit v6 on v5

--- a/solution.py
+++ b/solution.py
@@ -226,7 +226,7 @@
     for name, n in (
         ("x", nd - 1),
         ("w", nd - 1),
-        ("g", 8),
+        ("g", 12),
         ("s", nm),
         ("m", nm),
         ("b", nm),
@@ -256,7 +256,7 @@
     down = lax.rem(d + nd - 1, nd)
     across = lax.rem(d + 2, nd)
 
-    parts = (slice(0, 2), slice(2, 3))
+    parts = (slice(1, 2), slice(0, 1), slice(2, 3))
 
     def copies_g(part):
         at = parts[part]
@@ -403,6 +403,7 @@
     @pl.when(later)
     def _():
         start(bases["g"], copies_g(0))
+        start(bases["g"] + 4, copies_g(1))
 
     col = iota(perm.shape, 1)
     row = iota(perm.shape, 0)
@@ -530,8 +531,10 @@
         weights_small()
         prepare()
         pass_on(0)
-        start(bases["g"] + 4, copies_g(1))
+        pass_on(1)
+        start(bases["g"] + 8, copies_g(2))
         passed_on(0)
+        passed_on(1)
         arrived(recv_h, h_sem.at[0])
 
         @pl.when(sec == 1)
@@ -563,7 +566,7 @@
             acc += recv_t[i].astype(F32)
         send_u[...] = acc.astype(BF16)
         start(bases["u"], copies_u())
-        pass_on(1)
+        pass_on(2)
 
     loads[9].wait()
     per_head = iota((1, chan), 1) // head
@@ -734,7 +737,7 @@
 
     @pl.when(later)
     def _():
-        passed_on(1)
+        passed_on(2)
         out = jnp.zeros((rows, feat), F32)
         squares = jnp.zeros((rows, 1), F32)
         for i in range(nd):
@@ -783,7 +786,7 @@
         finish(bases["s"], copies_s(front))
         finish(bases["t"], copies_t())
         finish(bases["u"], copies_u())
-        for part in (0, 1):
+        for part in (0, 1, 2):
             finish(bases["g"] + 4 * part, copies_g(part))
             if nd == 4:
                 finish(bases["g"] + 4 * part + 2, copies_g2(part, 0))
@@ -863,7 +866,7 @@
         state_pool.reshape(slots_dev, chan, state),
         gate_gain,
     )
-    sends = 5 * nd + ratio + 3 * nm + 4
+    sends = 5 * nd + ratio + 3 * nm + 8
     dma = pltpu.SemaphoreType.DMA
     scratch = (
         [pltpu.SMEM(a.shape, a.dtype) for a in operands[:5]]
@@ -914,7 +917,7 @@
             dma((sends,)),
             dma((nd,)),
             dma((nd,)),
-            dma((2, 4)),
+            dma((3, 4)),
             dma((nm,)),
             dma((nd,)),
             dma((ratio,)),

time: 82.3 us -> 81.7 us (level)
  no operation moved by 1% of the time
where the time goes in v6:
time: 81.7 us; the launch traced here: 81.6 us
  Pallas kernels  81 us (99%)
    pallas_call x1, Pallas kernels, local(): pl.pallas_call(functools.partial(kernel, size), out_shape=(jax.ShapeDtype...  79.4 us

profile of v6, /device:TPU:129, one launch (start us, length us, event | category | flops | bytes accessed | tf_op | source)
XLA Modules:
  0.0 81.6 jit_solution(17024894102350265493)
XLA Ops:
  0.6 79.4 %shard_map.158 = (bf16[16,160]{1,0:T(8,128)(2,1)S(1)}, f32[16,320,128]{2,1,0:T(8,128)S(1)}) custom-call(s32[16]{0:T(128)} %len_h.1, s32[16]{0:T(128)} %slot_h.1, f32[1,5]{1,0:T(1,128)} %rate_h.1, f32[1,5]{1,0:T(1,128)} %bias_h.1, f32[1,5]{1,0:T(1,128)} %skip_h.1, bf16[16,160]{1,0:T(8,128)(2,1)} %hid_h.1, f32[1,2560]{1,0:T(1,128)} %gain_h.1, ...), custom_call_target="tpu_custom_call" | custom-call | tf_op jit(solution)/shard_map/pallas_call | solution.py:931
  80.1 1.6 %shard_map.159 = (bf16[16,160]{1,0:T(8,128)(2,1)}, f32[16,320,128]{2,1,0:T(8,128)}) custom-call(bf16[16,160]{1,0:T(8,128)(2,1)S(1)} %get-tuple-element.6.hid_v, f32[16,320,128]{2,1,0:T(8,128)S(1)} %get-tuple-element.7.st_v), custom_call_target="tpu_custom_call" | custom-call | tf_op jit(solution)/shard_map/pallas_call | solution.py:948

commit v7 on v6

--- a/solution.py
+++ b/solution.py
@@ -738,6 +738,17 @@
     @pl.when(later)
     def _():
         passed_on(2)
+        finish(bases["s"], copies_s(front))
+        finish(bases["t"], copies_t())
+        finish(bases["u"], copies_u())
+        for part in (0, 1, 2):
+            finish(bases["g"] + 4 * part, copies_g(part))
+            if nd == 4:
+                finish(bases["g"] + 4 * part + 2, copies_g2(part, 0))
+                finish(bases["g"] + 4 * part + 3, copies_g2(part, 1))
+        for n, k in enumerate(far_first):
+            for p in range(pairs):
+                finish(bases["m"] + n * ratio + 2 * p, copies_m_later(k, p))
         out = jnp.zeros((rows, feat), F32)
         squares = jnp.zeros((rows, 1), F32)
         for i in range(nd):
@@ -783,17 +794,6 @@
 
     @pl.when(later)
     def _():
-        finish(bases["s"], copies_s(front))
-        finish(bases["t"], copies_t())
-        finish(bases["u"], copies_u())
-        for part in (0, 1, 2):
-            finish(bases["g"] + 4 * part, copies_g(part))
-            if nd == 4:
-                finish(bases["g"] + 4 * part + 2, copies_g2(part, 0))
-                finish(bases["g"] + 4 * part + 3, copies_g2(part, 1))
-        for n, k in enumerate(far_first):
-            for p in range(pairs):
-                finish(bases["m"] + n * ratio + 2 * p, copies_m_later(k, p))
         finish(bases["b"], copies_b_later())
 
         @pl.when(more)

time: 81.7 us -> 81.6 us (level)
  no operation moved by 1% of the time
where the time goes in v7:
time: 81.6 us
  Pallas kernels  80.9 us (99%)
    pallas_call x1, Pallas kernels, local(): pl.pallas_call(functools.partial(kernel, size), out_shape=(jax.ShapeDtype...  79.4 us

profile of v7, /device:TPU:129, one launch (start us, length us, event | category | flops | bytes accessed | tf_op | source)
XLA Modules:
  0.0 81.6 jit_solution(4923692991220377033)
XLA Ops:
  0.6 79.4 %shard_map.158 = (bf16[16,160]{1,0:T(8,128)(2,1)S(1)}, f32[16,320,128]{2,1,0:T(8,128)S(1)}) custom-call(s32[16]{0:T(128)} %len_h.1, s32[16]{0:T(128)} %slot_h.1, f32[1,5]{1,0:T(1,128)} %rate_h.1, f32[1,5]{1,0:T(1,128)} %bias_h.1, f32[1,5]{1,0:T(1,128)} %skip_h.1, bf16[16,160]{1,0:T(8,128)(2,1)} %hid_h.1, f32[1,2560]{1,0:T(1,128)} %gain_h.1, ...), custom_call_target="tpu_custom_call" | custom-call | tf_op jit(solution)/shard_map/pallas_call | solution.py:931
  80.0 1.6 %shard_map.159 = (bf16[16,160]{1,0:T(8,128)(2,1)}, f32[16,320,128]{2,1,0:T(8,128)}) custom-call(bf16[16,160]{1,0:T(8,128)(2,1)S(1)} %get-tuple-element.6.hid_v, f32[16,320,128]{2,1,0:T(8,128)S(1)} %get-tuple-element.7.st_v), custom_call_target="tpu_custom_call" | custom-call | tf_op jit(solution)/shard_map/pallas_call | solution.py:948
